TPU v7x, 32 devices: a whole 2x2x4 slice. The times are simulated.
32 devices in a mesh: grp: 2 (over x), head: 16 (over z, y, core).
Axes of the slice: x: 2, y: 2, z: 4, core: 2. Of those that a mesh axis runs over, the one named last changes fastest.
Arguments:
- queries: bfloat16 [2048, 2, 16, 256], P('head', 'grp'), parts along dimension 1, may hold values from -12 to 12
- new_kv: bfloat16 [2048, 2, 2, 512], P('head', 'grp'), parts along dimension 1, may hold values from -4 to 4
- cache: bfloat16 [32, 256, 512], P(('grp', 'head')), parts along dimension 0, may hold values from -12 to 12
- resid: bfloat16 [2048, 2, 2048], P('head', 'grp'), parts along dimension 1, may hold values from -6 to 6
- w_out: bfloat16 [16, 256, 2048], P(None, 'head'), may hold values from -0.375 to 0.375
- norm_gain: float32 [2048], replicated, may hold values from 0.1 to 1.9
- expert_ids: int32 [2048, 2, 2], P('head', 'grp'), parts along dimension 1, may hold values from 0 to 15, all different within a row; in each aligned block of 128 rows (0 to 127, 128 to 255, ..., all dimensions but the last counted through in order) at most 32 rows name the same one
- expert_gates: float32 [2048, 2, 2], P('head', 'grp'), parts along dimension 1, may hold values from 0.2 to 1
- w_in: bfloat16 [16, 2048, 1024], P('head'), may hold values from -0.125 to 0.125
- w_down: bfloat16 [16, 512, 2048], P('head'), may hold values from -0.25 to 0.25
Outputs:
- layer_out: bfloat16 [2048, 2, 2048], P('head', 'grp'), parts along dimension 1
There are 2 independent parts, one for each index of `grp`. A program takes and returns all parts, laid end to end along the dimension named above; an argument that names none is the same for every part. Nothing has to cross between parts.
Inputs may be any that keep to these rules, and one draw needn't show every extreme that they name: `expert_ids`: rows are taken in order over positions and then sequences; in each aligned block of 128 such rows (the rows of one device) no expert is named by more than 32 rows, a bound that some block reaches. A row names 2 different experts.
All inputs are finite; a program needn't handle non-finite values.
Results may differ from a plain program's by a relative error of at most 0.009.
Values may be sent and summed in bfloat16 or wider, within the bound.
A program may use at most 128 MiB of HBM per device.

v0:
```python
import jax
import jax.numpy as jnp
from jax import lax
from jax.sharding import PartitionSpec as P

eps_norm = 1e-06


def partner_2(value, axis, stride):
    mask = 2**stride
    pairs = [(source, source ^ mask) for source in range(lax.axis_size(axis))]
    return lax.ppermute(value, axis, pairs)


def attend(query_rows_all, new_keys, new_values, cached):
    length = query_rows_all.shape[0]
    head_width = query_rows_all.shape[1]
    block_rows = min(512, length)
    score_scale = head_width ** (-0.5)
    old_keys = cached[:, :head_width]
    old_values = cached[:, head_width:]
    key_positions = jnp.arange(length, dtype=jnp.int32)

    def one_block(first_row):
        query_rows = lax.dynamic_slice_in_dim(query_rows_all, first_row, block_rows, 0)
        old_scores = (
            jnp.dot(query_rows, old_keys.T, preferred_element_type=jnp.float32) * score_scale
        )
        new_scores = (
            jnp.dot(query_rows, new_keys.T, preferred_element_type=jnp.float32) * score_scale
        )
        row_positions = first_row + jnp.arange(block_rows, dtype=jnp.int32)
        allowed = key_positions[None, :] <= row_positions[:, None]
        new_scores = jnp.where(allowed, new_scores, -jnp.inf)
        row_max = jnp.maximum(jnp.max(old_scores, 1), jnp.max(new_scores, 1))[:, None]
        old_exp = jnp.exp(old_scores - row_max)
        new_exp = jnp.exp(new_scores - row_max)
        denominator = jnp.sum(old_exp, 1) + jnp.sum(new_exp, 1)
        weighted_sum = jnp.dot(
            old_exp.astype(jnp.bfloat16), old_values, preferred_element_type=jnp.float32
        )
        weighted_sum = weighted_sum + jnp.dot(
            new_exp.astype(jnp.bfloat16), new_values, preferred_element_type=jnp.float32
        )
        return (weighted_sum / denominator[:, None]).astype(jnp.bfloat16)

    starts = jnp.arange(length // block_rows) * block_rows
    return lax.map(one_block, starts).reshape(length, head_width)


def local(queries, new_kv, cache, resid, w_out, norm_gain, expert_ids, expert_gates, w_in, w_down):
    axis_count = lax.axis_size("head")
    local_rows = queries.shape[0]
    seq_count = queries.shape[1]
    head_count = queries.shape[2]
    head_width = queries.shape[3]
    pair_heads = new_kv.shape[2]
    group_size = head_count // pair_heads
    model_width = resid.shape[2]
    row_count = local_rows * seq_count
    query_slots = queries.reshape(local_rows, axis_count, head_width)
    pair_slots = jnp.broadcast_to(
        new_kv[:, :, :, None, :], (local_rows, seq_count, pair_heads, group_size, 2 * head_width)
    )
    pair_slots = pair_slots.reshape(local_rows, axis_count, 2 * head_width)
    head_queries = lax.all_to_all(query_slots, "head", split_axis=1, concat_axis=0, tiled=True)[
        :, 0
    ]
    head_pairs = lax.all_to_all(pair_slots, "head", split_axis=1, concat_axis=0, tiled=True)[:, 0]
    cache_rows = cache[0]
    for bit_number in range(group_size.bit_length() - 1):
        partner = partner_2(cache_rows, "head", bit_number)
        cache_rows = jnp.concatenate([cache_rows, partner], 0)
    attended = attend(
        head_queries, head_pairs[:, :head_width], head_pairs[:, head_width:], cache_rows
    )
    returned = lax.all_to_all(
        attended.reshape(attended.shape[0], 1, head_width),
        "head",
        split_axis=0,
        concat_axis=1,
        tiled=True,
    )
    attn_rows = returned.reshape(row_count, head_count * head_width)
    attn_heads = attn_rows.reshape(row_count, head_count, head_width)
    projected = jnp.einsum(
        "rhi,hid->rd",
        attn_heads,
        lax.all_gather(w_out, "head", axis=1, tiled=True),
        preferred_element_type=jnp.float32,
    )
    stream = resid.reshape(row_count, model_width).astype(jnp.float32) + projected
    normed = stream * lax.rsqrt(jnp.mean(stream * stream, 1, keepdims=True) + eps_norm) * norm_gain
    normed = normed.astype(jnp.bfloat16)
    top_count = expert_ids.shape[2]
    flat_ids = expert_ids.reshape(-1)
    local_experts = w_in.shape[0]
    experts = local_experts * axis_count
    capacity = max(2, 2 * row_count * top_count // experts)
    onehot = (flat_ids[:, None] == jnp.arange(experts, dtype=jnp.int32)[None, :]).astype(jnp.int32)
    earlier = jnp.cumsum(onehot, 0) - onehot
    slot_rank = jnp.sum(earlier * onehot, 1)
    target = flat_ids * capacity + slot_rank
    repeated = jnp.repeat(normed, top_count, axis=0)
    outgoing = jnp.zeros((experts * capacity, model_width), jnp.bfloat16).at[target].set(repeated)
    outgoing = outgoing.reshape(experts, 1, capacity, model_width)
    hidden_width = w_down.shape[1]
    inner_act = jnp.einsum(
        "esmd,edf->esmf",
        lax.all_to_all(outgoing, "head", split_axis=0, concat_axis=1, tiled=True),
        w_in,
        preferred_element_type=jnp.float32,
    )
    hidden = (jax.nn.silu(inner_act[..., :hidden_width]) * inner_act[..., hidden_width:]).astype(
        jnp.bfloat16
    )
    answered = jnp.einsum(
        "esmf,efd->esmd", hidden, w_down, preferred_element_type=jnp.float32
    ).astype(jnp.bfloat16)
    returned_rows = lax.all_to_all(answered, "head", split_axis=1, concat_axis=0, tiled=True)
    picked = returned_rows.reshape(experts * capacity, model_width)[target].astype(jnp.float32)
    weighted = picked * expert_gates.reshape(-1)[:, None]
    expert_sum = weighted.reshape(row_count, top_count, model_width).sum(1)
    return (stream + expert_sum).astype(jnp.bfloat16).reshape(local_rows, seq_count, model_width)


def solution(mesh):
    return jax.shard_map(
        local,
        mesh=mesh,
        in_specs=(
            P("head", "grp", None, None),
            P("head", "grp", None, None),
            P(("grp", "head"), None, None),
            P("head", "grp", None),
            P(None, "head", None),
            P(),
            P("head", "grp", None),
            P("head", "grp", None),
            P("head", None, None),
            P("head", None, None),
        ),
        out_specs=P("head", "grp", None),
        check_vma=False,
    )
```

profile of v0, /device:TPU:13, one launch (start us, length us, event | category | flops | bytes accessed | tf_op | source)
XLA Modules:
  0.0 386.2 jit_solution(4581564289091582553)
XLA Ops:
  9.7 6.5 %all-to-all-start.1 = ((bf16[128,16,512]{2,0,1:T(8,128)(2,1)}), bf16[128,16,512]{2,0,1:T(8,128)(2,1)}, u32[]{:S(2)}, u32[]{:S(2)}) async-start(bf16[128,16,512]{2,0,1:T(8,128)(2,1)} %bitcast.108), calls=%async_computation.1 | async-start | bytes 4194304 | tf_op jit(solution)/shard_map/all_to_all | solution.py:69
  18.5 33.3 %collective-permute-done.1 = bf16[512,512]{1,0:T(8,128)(2,1)S(1)} collective-permute-done((bf16[512,512]{1,0:T(8,128)(2,1)S(1)}, bf16[512,512]{1,0:T(8,128)(2,1)S(1)}, u32[]{:S(2)}, u32[]{:S(2)}) %collective-permute-start.1) | collective-permute-done | bytes 524320 | tf_op jit(solution)/shard_map/ppermute | solution.py:12
  52.8 4.1 %collective-permute-start.2 = (bf16[1024,512]{1,0:T(8,128)(2,1)}, bf16[1024,512]{1,0:T(8,128)(2,1)}, u32[]{:S(2)}, u32[]{:S(2)}) collective-permute-start(bf16[1024,512]{1,0:T(8,128)(2,1)} %pad_maximum_fusion.1), channel_id=1, source_target_pairs={{0,4},{1,5},{2,6},{3,7},{4,0},{5,1},{6,2},{7,3},{8,12},{9,13},{10,... | collective-permute-start | bytes 3145736 | tf_op jit(solution)/shard_map/ppermute | solution.py:12
  56.9 2.6 copy.42
  59.5 38.3 %all-to-all-done.1 = bf16[128,16,512]{2,0,1:T(8,128)(2,1)} async-done(((bf16[128,16,512]{2,0,1:T(8,128)(2,1)}), bf16[128,16,512]{2,0,1:T(8,128)(2,1)}, u32[]{:S(2)}, u32[]{:S(2)}) %all-to-all-start.1) | async-done | bytes 2097184 | tf_op jit(solution)/shard_map/all_to_all | solution.py:69
  97.7 4.4 %all-to-all-start = ((bf16[128,16,256]{2,0,1:T(8,128)(2,1)}), bf16[128,16,256]{2,0,1:T(8,128)(2,1)}, u32[]{:S(2)}, u32[]{:S(2)}) async-start(bf16[128,16,256]{2,0,1:T(8,128)(2,1)} %bitcast.95), calls=%async_computation | async-start | bytes 2097152 | tf_op jit(solution)/shard_map/all_to_all | solution.py:66
  102.2 20.2 %collective-permute-done.2 = bf16[1024,512]{1,0:T(8,128)(2,1)} collective-permute-done((bf16[1024,512]{1,0:T(8,128)(2,1)}, bf16[1024,512]{1,0:T(8,128)(2,1)}, u32[]{:S(2)}, u32[]{:S(2)}) %collective-permute-start.2) | collective-permute-done | bytes 1048608 | tf_op jit(solution)/shard_map/ppermute | solution.py:12
  124.8 3.0 fusion.57
  127.9 24.4 %all-to-all-done = bf16[128,16,256]{2,0,1:T(8,128)(2,1)} async-done(((bf16[128,16,256]{2,0,1:T(8,128)(2,1)}), bf16[128,16,256]{2,0,1:T(8,128)(2,1)}, u32[]{:S(2)}, u32[]{:S(2)}) %all-to-all-start) | async-done | bytes 1048608 | tf_op jit(solution)/shard_map/all_to_all | solution.py:66
  152.3 45.5 %while.11 = (s32[]{:T(128)}, bf16[4,512,256]{2,1,0:T(8,128)(2,1)}, s32[4]{0:T(128)S(1)}, bf16[2048,256]{1,0:T(8,128)(2,1)}, bf16[2048,256]{1,0:T(8,128)(2,1)S(1)...) while((s32[]{:T(128)}, bf16[4,512,256]{2,1,0:T(8,128)(2,1)}, ...), condition=%wide.region_5.6_spmd.clone, body=%wide.region_0.5_spmd.clone.sunk | while | flops 2164653568 | bytes 39617248 | solution.py:48
  155.4 2.3 fusion.81
  166.8 2.3 fusion.81
  178.2 2.3 fusion.81
  180.5 1.8 multiply_reduce_fusion.4
  189.6 2.3 fusion.81
  191.9 1.8 multiply_reduce_fusion.4
  198.3 2.7 reduce.2
  202.1 4.7 %all-to-all-start.2 = ((bf16[16,2,16384]{2,1,0:T(2,128)(2,1)}), bf16[16,2,16384]{2,1,0:T(2,128)(2,1)S(1)}, u32[]{:S(2)}, u32[]{:S(2)}) async-start(bf16[16,2,16384]{2,1,0:T(2,128)(2,1)} %reshape.162), calls=%async_computation.2 | async-start | bytes 2097152 | tf_op jit(solution)/shard_map/all_to_all | solution.py:77
  208.5 23.3 %all-to-all-done.2 = bf16[16,2,16384]{2,1,0:T(2,128)(2,1)S(1)} async-done(((bf16[16,2,16384]{2,1,0:T(2,128)(2,1)}), bf16[16,2,16384]{2,1,0:T(2,128)(2,1)S(1)}, u32[]{:S(2)}, u32[]{:S(2)}) %all-to-all-start.2) | async-done | bytes 1048608 | tf_op jit(solution)/shard_map/all_to_all | solution.py:77
  231.7 3.5 reshape.163
  235.2 2.8 copy.38
  237.9 8.6 %multiply_reduce_fusion.2 = (f32[128]{0:T(128)S(1)}, f32[128,2048]{1,0:T(8,128)S(1)}) fusion(bf16[128,16,256]{2,0,1:T(8,128)(2,1)} %bitcast.110, bf16[16,256,2048]{2,1,0:T(8,128)(2,1)} %all-gather.2.cloned.1.call-done, bf16[128,1,2048]{2,0,1:T(8,128)(2,1)} %param.15), kind=kOutput, calls=%fused_computation.46 | convolution fusion | flops 2148532224 | bytes 19399168 | tf_op jit(solution)/shard_map/rhi,hid->rd/dot_general | solution.py:86
  248.3 2.3 reshape.152
  250.6 4.4 %scatter_custom_fusion = bf16[512,2048]{1,0:T(8,128)(2,1)} fusion(s32[256]{0:T(256)S(1)} %bitcast.116, bf16[256,2048]{1,0:T(8,128)(2,1)} %reshape.152, bf16[]{:T(256)} %constant.7.clone.1), kind=kCustom, calls=%fused_computation.47 | custom fusion | bytes 2097664 | tf_op jit(solution)/shard_map/scatter | solution.py:105
  255.0 52.4 %all_to_all.66 = bf16[16,1,32,2048]{3,2,1,0:T(8,128)(2,1)S(1)} all-to-all(bf16[16,1,32,2048]{3,2,1,0:T(8,128)(2,1)} %bitcast.109), channel_id=1, replica_groups=mesh['grp'=2,'head'=16] {'head'}, dimensions={0} | all-to-all | bytes 4194304 | tf_op jit(solution)/shard_map/all_to_all | solution.py:110
  307.4 2.3 fusion.40
  309.8 2.6 fusion.36
  312.3 5.2 %all-to-all-start.4 = ((bf16[1,16,32,2048]{3,2,0,1:T(8,128)(2,1)}), bf16[1,16,32,2048]{3,2,0,1:T(8,128)(2,1)}, u32[]{:S(2)}, u32[]{:S(2)}) async-start(bf16[1,16,32,2048]{3,2,0,1:T(8,128)(2,1)} %fusion.36), calls=%async_computation.4 | async-start | bytes 4194304 | tf_op jit(solution)/shard_map/all_to_all | solution.py:120
  317.6 47.4 %all-to-all-done.4 = bf16[1,16,32,2048]{3,2,0,1:T(8,128)(2,1)} async-done(((bf16[1,16,32,2048]{3,2,0,1:T(8,128)(2,1)}), bf16[1,16,32,2048]{3,2,0,1:T(8,128)(2,1)}, u32[]{:S(2)}, u32[]{:S(2)}) %all-to-all-start.4) | async-done | bytes 2097184 | tf_op jit(solution)/shard_map/all_to_all | solution.py:120
  365.0 5.2 %gather_fusion = bf16[256,2048]{1,0:T(8,128)(2,1)} fusion(bf16[512,2048]{1,0:T(8,128)(2,1)} %bitcast.30, s32[1024]{0:T(1024)S(1)} %pad_clamp_fusion), kind=kCustom, calls=%fused_computation | custom fusion | bytes 2098176 | tf_op jit(solution)/shard_map/gather | solution.py:121
  370.2 3.4 reshape.139
  373.6 4.8 %multiply_reduce_fusion.1 = f32[128,2048]{1,0:T(8,128)S(1)} fusion(f32[128,2,2048]{2,1,0:T(2,128)} %reshape.139, f32[128,2]{1,0:T(8,128)S(1)} %copy.37), kind=kLoop, calls=%fused_computation.38 | loop fusion | flops 786432 | bytes 3146752 | tf_op jit(solution)/shard_map/reduce_sum | solution.py:123
  (93 shorter events, 39.9 us)
Async XLA Ops:
  6.5 303.2 %copy-start = (bf16[1,512,2048]{2,1,0:T(8,128)(2,1)S(1)}, bf16[1,512,2048]{2,1,0:T(8,128)(2,1)}, u32[]{:S(2)}) copy-start(bf16[1,512,2048]{2,1,0:T(8,128)(2,1)} %param.21) | copy-start | bytes 6291460
  6.5 9.7 %copy-start.1 = (bf16[1,256,512]{2,1,0:T(8,128)(2,1)S(1)}, bf16[1,256,512]{2,1,0:T(8,128)(2,1)}, u32[]{:S(2)}) copy-start(bf16[1,256,512]{2,1,0:T(8,128)(2,1)} %param.14) | copy-start | bytes 786436
  6.5 231.4 %all-gather.2.cloned.1.call-start = ((), (), s32[]{:S(2)}) async-start(), calls=%async_computation.5 | async-start | bytes 17825792 | tf_op jit(solution)/shard_map/all_gather | solution.py:89
  9.7 88.0 %all-to-all-start.1 = ((bf16[128,16,512]{2,0,1:T(8,128)(2,1)}), bf16[128,16,512]{2,0,1:T(8,128)(2,1)}, u32[]{:S(2)}, u32[]{:S(2)}) async-start(bf16[128,16,512]{2,0,1:T(8,128)(2,1)} %bitcast.108), calls=%async_computation.1 | async-start | bytes 4194304 | tf_op jit(solution)/shard_map/all_to_all | solution.py:69
  16.3 1.8 collective-permute-start
  18.1 33.7 %collective-permute-start.1 = (bf16[512,512]{1,0:T(8,128)(2,1)S(1)}, bf16[512,512]{1,0:T(8,128)(2,1)S(1)}, u32[]{:S(2)}, u32[]{:S(2)}) collective-permute-start(bf16[512,512]{1,0:T(8,128)(2,1)S(1)} %pad_maximum_fusion.2), channel_id=1, source_target_pairs={{0,2},{1,3},{2,0},{3,1},{4,6},{5,7},{6,4},{7,5},{8,10},{9,11},{10,... | collective-permute-start | bytes 1572872 | tf_op jit(solution)/shard_map/ppermute | solution.py:12
  52.8 69.5 %collective-permute-start.2 = (bf16[1024,512]{1,0:T(8,128)(2,1)}, bf16[1024,512]{1,0:T(8,128)(2,1)}, u32[]{:S(2)}, u32[]{:S(2)}) collective-permute-start(bf16[1024,512]{1,0:T(8,128)(2,1)} %pad_maximum_fusion.1), channel_id=1, source_target_pairs={{0,4},{1,5},{2,6},{3,7},{4,0},{5,1},{6,2},{7,3},{8,12},{9,13},{10,... | collective-permute-start | bytes 3145736 | tf_op jit(solution)/shard_map/ppermute | solution.py:12
  97.7 54.5 %all-to-all-start = ((bf16[128,16,256]{2,0,1:T(8,128)(2,1)}), bf16[128,16,256]{2,0,1:T(8,128)(2,1)}, u32[]{:S(2)}, u32[]{:S(2)}) async-start(bf16[128,16,256]{2,0,1:T(8,128)(2,1)} %bitcast.95), calls=%async_computation | async-start | bytes 2097152 | tf_op jit(solution)/shard_map/all_to_all | solution.py:66
  159.5 1.4 copy-start.2
  160.9 1.2 copy-start.3
  170.9 1.4 copy-start.2
  172.3 1.2 copy-start.3
  182.3 1.4 copy-start.2
  183.7 1.2 copy-start.3
  193.7 1.4 copy-start.2
  195.1 1.2 copy-start.3
  197.8 9.1 %copy-start.5 = (s32[128,1,2]{0,2,1:T(2,128)S(1)}, s32[128,1,2]{0,2,1:T(2,128)}, u32[]{:S(2)}) copy-start(s32[128,1,2]{0,2,1:T(2,128)} %param.18) | copy-start | bytes 3076
  202.1 29.6 %all-to-all-start.2 = ((bf16[16,2,16384]{2,1,0:T(2,128)(2,1)}), bf16[16,2,16384]{2,1,0:T(2,128)(2,1)S(1)}, u32[]{:S(2)}, u32[]{:S(2)}) async-start(bf16[16,2,16384]{2,1,0:T(2,128)(2,1)} %reshape.162), calls=%async_computation.2 | async-start | bytes 2097152 | tf_op jit(solution)/shard_map/all_to_all | solution.py:77
  237.9 8.6 %copy-start.4 = (f32[2048]{0:T(1024)S(1)}, f32[2048]{0:T(1024)}, u32[]{:S(2)}) copy-start(f32[2048]{0:T(1024)} %param.17) | copy-start | bytes 24580
  255.0 52.4 %copy-start.7 = (bf16[1,2048,1024]{2,1,0:T(8,128)(2,1)S(1)}, bf16[1,2048,1024]{2,1,0:T(8,128)(2,1)}, u32[]{:S(2)}) copy-start(bf16[1,2048,1024]{2,1,0:T(8,128)(2,1)} %param.20) | copy-start | bytes 12582916
  312.3 5.2 %copy-start.6 = (f32[128,1,2]{0,2,1:T(2,128)S(1)}, f32[128,1,2]{0,2,1:T(2,128)}, u32[]{:S(2)}) copy-start(f32[128,1,2]{0,2,1:T(2,128)} %param.19) | copy-start | bytes 3076
  312.3 52.7 %all-to-all-start.4 = ((bf16[1,16,32,2048]{3,2,0,1:T(8,128)(2,1)}), bf16[1,16,32,2048]{3,2,0,1:T(8,128)(2,1)}, u32[]{:S(2)}, u32[]{:S(2)}) async-start(bf16[1,16,32,2048]{3,2,0,1:T(8,128)(2,1)} %fusion.36), calls=%async_computation.4 | async-start | bytes 4194304 | tf_op jit(solution)/shard_map/all_to_all | solution.py:120
Sparse Core Ops, SparseCore 0:
  9.5 185.4 all-gather.1
where the time goes:
time: 388 us; the launch traced here: 386 us
  waiting for transfers between devices  189 us (49%)
  blocking collectives  52.4 us (14%)
  matrix products  39.2 us (10%)
  local copies, waits for them, and re-layouts  38.8 us (10%)
  starting transfers between devices  25.8 us (7%)
  other arithmetic  19.9 us (5%)
  between operations  13.5 us (3%)
  loops' own time  7.86 us (2%)
    ppermute x3, waiting for transfers between devices, partner_2(): return lax.ppermute(value, axis, pairs)  54.8 us
    all_to_all x1, blocking collectives, local(): lax.all_to_all(outgoing, 'head', split_axis=0, concat_axis=1, tiled=True)  52.4 us
    all_to_all x1, waiting for transfers between devices, local(): lax.all_to_all(answered, 'head', split_axis=1, concat_axis=0, tiled=True)  47.4 us
    all_to_all x1, waiting for transfers between devices, local(): lax.all_to_all(pair_slots, 'head', split_axis=1, concat_axis=0, tiled=True)  38.3 us
    all_to_all x1, waiting for transfers between devices, local(): lax.all_to_all(query_slots, 'head', split_axis=1, concat_axis=0, tiled=True)  24.4 us
    all_to_all x1, waiting for transfers between devices, local(): lax.all_to_all(attended.reshape(attended.shape[0], 1, head_width), 'head'...  23.3 us
    unnamed x17, local copies, waits for them, and re-layouts  10 us
    dot_general x4, matrix products, one_block(): jnp.dot(query_rows, new_keys.T, preferred_element_type=jnp.float32)  9.17 us
  transfers between devices with their start and end apart: 8, of which 7 were waited for; matrix products, arithmetic and copies ran while one was open for 16% of the time, Pallas kernels for 0%

commit v1 on v0

v1 whole, which is shorter than its diff:
```python
import functools

import jax
import jax.numpy as jnp
from jax import lax
from jax.experimental import pallas as pl
from jax.sharding import PartitionSpec as P

eps_norm = 1e-06


def attend_kernel(query_ref, cache_ref, new_ref, out_ref, *, block, old_block):
    head_width = query_ref.shape[1]
    step = pl.program_id(0)
    query_rows = query_ref[...] * jnp.asarray(head_width ** (-0.5), query_ref.dtype)

    def fold(carry, keys, values, mask):
        top, total, weighted = carry
        scores = lax.dot_general(
            query_rows, keys, (((1,), (1,)), ((), ())), preferred_element_type=jnp.float32
        )
        if mask is not None:
            scores = jnp.where(mask, scores, -jnp.inf)
        new_top = jnp.maximum(top, jnp.max(scores, 1, keepdims=True))
        exps = jnp.exp(scores - new_top)
        shrink = jnp.exp(top - new_top)
        total = total * shrink + jnp.sum(exps, 1, keepdims=True)
        weighted = weighted * shrink + jnp.dot(
            exps.astype(jnp.bfloat16), values, preferred_element_type=jnp.float32
        )
        return new_top, total, weighted

    rows = query_rows.shape[0]
    carry = (
        jnp.full((rows, 1), -jnp.inf, jnp.float32),
        jnp.zeros((rows, 1), jnp.float32),
        jnp.zeros((rows, head_width), jnp.float32),
    )
    row_at = lax.broadcasted_iota(jnp.int32, (rows, block), 0)
    col_at = lax.broadcasted_iota(jnp.int32, (rows, block), 1)
    here = pl.ds(step * block, block)
    carry = fold(
        carry, new_ref[here, :head_width], new_ref[here, head_width:], col_at <= row_at
    )
    for first in range(0, cache_ref.shape[0], old_block):
        part = pl.ds(first, old_block)
        carry = fold(carry, cache_ref[part, :head_width], cache_ref[part, head_width:], None)

    def earlier(index, carry):
        part = pl.ds(index * block, block)
        return fold(carry, new_ref[part, :head_width], new_ref[part, head_width:], None)

    top, total, weighted = lax.fori_loop(0, step, earlier, carry)
    out_ref[...] = (weighted / total).astype(out_ref.dtype)


def attend(queries, new_pairs, cached):
    length, head_width = queries.shape
    block = min(512, length)
    old_block = min(1024, cached.shape[0])
    return pl.pallas_call(
        functools.partial(attend_kernel, block=block, old_block=old_block),
        grid=(length // block,),
        in_specs=[
            pl.BlockSpec((block, head_width), lambda i: (i, 0)),
            pl.BlockSpec(cached.shape, lambda i: (0, 0)),
            pl.BlockSpec(new_pairs.shape, lambda i: (0, 0)),
        ],
        out_specs=pl.BlockSpec((block, head_width), lambda i: (i, 0)),
        out_shape=jax.ShapeDtypeStruct((length, head_width), jnp.bfloat16),
        cost_estimate=pl.CostEstimate(
            flops=4 * length * head_width * (length // 2 + cached.shape[0]),
            bytes_accessed=8 * length * head_width * 2,
            transcendentals=length * (length // 2 + cached.shape[0]),
        ),
    )(queries, cached, new_pairs)


def local(queries, new_kv, cache, resid, w_out, norm_gain, expert_ids, expert_gates, w_in, w_down):
    axis_count = lax.axis_size("head")
    local_rows = queries.shape[0]
    seq_count = queries.shape[1]
    head_count = queries.shape[2]
    head_width = queries.shape[3]
    pair_heads = new_kv.shape[2]
    group_size = head_count // pair_heads
    model_width = resid.shape[2]
    row_count = local_rows * seq_count
    slots = seq_count * pair_heads
    across = [[c * group_size + j for c in range(slots)] for j in range(group_size)]
    inside = [[c * group_size + j for j in range(group_size)] for c in range(slots)]
    query_slots = queries.reshape(local_rows, axis_count, head_width).transpose(1, 0, 2)
    pair_slots = new_kv.reshape(local_rows, slots, 2 * head_width).transpose(1, 0, 2)
    pair_slots = lax.all_to_all(
        pair_slots, "head", split_axis=0, concat_axis=0, axis_index_groups=across, tiled=True
    )
    cache_rows = lax.all_gather(cache[0], "head", axis=0, axis_index_groups=inside, tiled=True)
    pairs = lax.all_gather(pair_slots, "head", axis=0, axis_index_groups=inside, tiled=False)
    pairs = pairs.transpose(1, 0, 2, 3).reshape(axis_count * local_rows, 2 * head_width)
    head_queries = lax.all_to_all(query_slots, "head", split_axis=0, concat_axis=0, tiled=True)
    attended = attend(head_queries.reshape(-1, head_width), pairs, cache_rows)
    returned = lax.all_to_all(
        attended.reshape(axis_count, local_rows, head_width),
        "head",
        split_axis=0,
        concat_axis=0,
        tiled=True,
    )
    attn_rows = returned.reshape(seq_count, head_count, local_rows, head_width)
    attn_rows = attn_rows.transpose(2, 0, 1, 3).reshape(row_count, head_count * head_width)
    w_full = lax.all_gather(w_out, "head", axis=1, tiled=True)
    projected = jnp.dot(
        attn_rows,
        w_full.reshape(head_count * head_width, model_width),
        preferred_element_type=jnp.float32,
    )
    stream = resid.reshape(row_count, model_width).astype(jnp.float32) + projected
    normed = stream * lax.rsqrt(jnp.mean(stream * stream, 1, keepdims=True) + eps_norm) * norm_gain
    normed = normed.astype(jnp.bfloat16)
    top_count = expert_ids.shape[2]
    flat_ids = expert_ids.reshape(-1)
    local_experts = w_in.shape[0]
    experts = local_experts * axis_count
    capacity = max(2, 2 * row_count * top_count // experts)
    onehot = (flat_ids[:, None] == jnp.arange(experts, dtype=jnp.int32)[None, :]).astype(jnp.int32)
    earlier = jnp.cumsum(onehot, 0) - onehot
    slot_rank = jnp.sum(earlier * onehot, 1)
    target = flat_ids * capacity + slot_rank
    repeated = jnp.repeat(normed, top_count, axis=0)
    outgoing = jnp.zeros((experts * capacity, model_width), jnp.bfloat16).at[target].set(repeated)
    outgoing = outgoing.reshape(experts, 1, capacity, model_width)
    hidden_width = w_down.shape[1]
    inner_act = jnp.einsum(
        "esmd,edf->esmf",
        lax.all_to_all(outgoing, "head", split_axis=0, concat_axis=1, tiled=True),
        w_in,
        preferred_element_type=jnp.float32,
    )
    hidden = (jax.nn.silu(inner_act[..., :hidden_width]) * inner_act[..., hidden_width:]).astype(
        jnp.bfloat16
    )
    answered = jnp.einsum(
        "esmf,efd->esmd", hidden, w_down, preferred_element_type=jnp.float32
    ).astype(jnp.bfloat16)
    returned_rows = lax.all_to_all(answered, "head", split_axis=1, concat_axis=0, tiled=True)
    picked = returned_rows.reshape(experts * capacity, model_width)[target].astype(jnp.float32)
    weighted = picked * expert_gates.reshape(-1)[:, None]
    expert_sum = weighted.reshape(row_count, top_count, model_width).sum(1)
    return (stream + expert_sum).astype(jnp.bfloat16).reshape(local_rows, seq_count, model_width)


def solution(mesh):
    return jax.shard_map(
        local,
        mesh=mesh,
        in_specs=(
            P("head", "grp", None, None),
            P("head", "grp", None, None),
            P(("grp", "head"), None, None),
            P("head", "grp", None),
            P(None, "head", None),
            P(),
            P("head", "grp", None),
            P("head", "grp", None),
            P("head", None, None),
            P("head", None, None),
        ),
        out_specs=P("head", "grp", None),
        check_vma=False,
    )
```

time: 388 us -> 376 us (0.969)
  waiting for transfers between devices: 189 us -> 216 us
  matrix products: 39.2 us -> 13.5 us
  Pallas kernels: 0 us -> 19.1 us
  other arithmetic: 19.9 us -> 6.66 us
  local copies, waits for them, and re-layouts: 38.8 us -> 25.7 us
  blocking collectives: 52.4 us -> 63.6 us
  loops' own time: 7.86 us -> 0 us
  starting transfers between devices: 25.8 us -> 18.3 us
    all_gather x1 -> x3, waiting for transfers between devices: 0.01 us -> 125 us  [the longest x1 76.5 us: local(): w_full = lax.all_gather(w_out, 'head', axis=1, tiled=True)]
    ppermute x3 -> x0, waiting for transfers between devices: 54.8 us -> none  [partner_2(): return lax.ppermute(value, axis, pairs)]
    all_to_all x3 -> x2, waiting for transfers between devices: 85.9 us -> 42.2 us  [the longest x1 42.2 us: local(): lax.all_to_all(attended.reshape(axis_count, local_rows, head_width), 'hea...]
    dot_general x17 -> x1, matrix products: 34.2 us -> 8.56 us  [local(): jnp.dot(attn_rows, w_full.reshape(head_count * head_width, model_width),...]
    pallas_call x0 -> x1, Pallas kernels: none -> 19.1 us  [attend(): pl.pallas_call(functools.partial(attend_kernel, block=block, old_block=ol...]
    all_to_all x0 -> x1, blocking collectives: none -> 9.5 us  [local(): lax.all_to_all(pair_slots, 'head', split_axis=0, concat_axis=0, axis_inde...]
    another operation x1 -> x0, loops' own time: 7.86 us -> none  [attend(): return lax.map(one_block, starts).reshape(length, head_width)]
    unnamed x17 -> x19, local copies, waits for them, and re-layouts: 10 us -> 2.61 us
  transfers between devices with their start and end apart: 8 -> 6, of which waited for: 7 -> 5; matrix products, arithmetic and copies ran while one was open for 16% -> 2% of each run, Pallas kernels for 0% -> 5%
where the time goes in v1:
time: 376 us
  waiting for transfers between devices  216 us (57%)
  blocking collectives  63.6 us (17%)
  local copies, waits for them, and re-layouts  25.7 us (7%)
  Pallas kernels  19.1 us (5%)
  starting transfers between devices  18.3 us (5%)
  matrix products  13.5 us (4%)
  between operations  13.2 us (4%)
  other arithmetic  6.66 us (2%)
    all_gather x1, waiting for transfers between devices, local(): w_full = lax.all_gather(w_out, 'head', axis=1, tiled=True)  76.5 us
    all_to_all x1, blocking collectives, local(): lax.all_to_all(outgoing, 'head', split_axis=0, concat_axis=1, tiled=True)  54.1 us
    all_to_all x1, waiting for transfers between devices, local(): lax.all_to_all(answered, 'head', split_axis=1, concat_axis=0, tiled=True)  47.4 us
    all_to_all x1, waiting for transfers between devices, local(): lax.all_to_all(attended.reshape(axis_count, local_rows, head_width), 'hea...  42.2 us
    all_gather x1, waiting for transfers between devices, local(): lax.all_gather(pair_slots, 'head', axis=0, axis_index_groups=inside, tile...  27.4 us
    all_gather x1, waiting for transfers between devices, local(): lax.all_gather(cache[0], 'head', axis=0, axis_index_groups=inside, tiled=...  21.1 us
    pallas_call x1, Pallas kernels, attend(): pl.pallas_call(functools.partial(attend_kernel, block=block, old_block=ol...  19.1 us
    all_to_all x1, blocking collectives, local(): lax.all_to_all(pair_slots, 'head', split_axis=0, concat_axis=0, axis_inde...  9.5 us
  transfers between devices with their start and end apart: 6, of which 5 were waited for; matrix products, arithmetic and copies ran while one was open for 2% of the time, Pallas kernels for 5%

profile of v1, /device:TPU:13, one launch (start us, length us, event | category | flops | bytes accessed | tf_op | source)
XLA Modules:
  0.0 375.9 jit_solution(2618480422894461488)
XLA Ops:
  6.5 1.1 copy.37
  7.7 9.5 %all_to_all.33 = bf16[2,128,512]{2,1,0:T(8,128)(2,1)} all-to-all(bf16[2,128,512]{2,1,0:T(8,128)(2,1)S(1)} %bitcast.91), channel_id=1, replica_groups={{0,8},{1,9},{2,10},{3,11},{4,12},{5,13},{6,14},{7,15},{16,24},{17,25},{..., dimensions={0} | all-to-all | bytes 524288 | tf_op jit(solution)/shard_map/all_to_all | solution.py:94
  17.2 0.7 all-gather.8.cloned.1.call-update
  18.0 0.7 all-gather.6.cloned.1.call-update
  18.7 1.3 copy.36
  20.0 7.3 %all-to-all-start = ((bf16[16,128,256]{2,1,0:T(8,128)(2,1)}), bf16[16,128,256]{2,1,0:T(8,128)(2,1)S(1)}, u32[]{:S(2)}, u32[]{:S(2)}) async-start(bf16[16,128,256]{2,1,0:T(8,128)(2,1)} %bitcast.82), calls=%async_computation | async-start | bytes 2097152 | tf_op jit(solution)/shard_map/all_to_all | solution.py:100
  27.3 27.4 %all-gather.10.cloned.1.call-done = bf16[16,128,512]{2,1,0:T(8,128)(2,1)} async-done(((bf16[2,128,512]{2,1,0:T(8,128)(2,1)}), bf16[16,128,512]{2,1,0:T(8,128)(2,1)}) %all-gather.10.cloned.1.call-update) | async-done | bytes 2097168 | tf_op jit(solution)/shard_map/all_gather | solution.py:98
  54.7 3.1 copy.24
  57.8 21.1 %all-gather.8.cloned.1.call-done = bf16[1,2048,512]{2,1,0:T(8,128)(2,1)} async-done(((bf16[1,256,512]{2,1,0:T(8,128)(2,1)}), bf16[1,2048,512]{2,1,0:T(8,128)(2,1)}) %all-gather.8.cloned.1.call-update) | async-done | bytes 2097168 | tf_op jit(solution)/shard_map/all_gather | solution.py:97
  78.9 19.1 %shard_map.100 = bf16[2048,256]{1,0:T(8,128)(2,1)} custom-call(bf16[2048,256]{1,0:T(8,128)(2,1)} %bitcast.89, bf16[2048,512]{1,0:T(8,128)(2,1)} %bitcast.96, bf16[2048,512]{1,0:T(8,128)(2,1)} %bitcast.88), custom_call_target="tpu_custom_call" | custom-call | flops 6442450944 | bytes 8388608 | tf_op jit(solution)/shard_map/pallas_call | solution.py:61
  98.0 2.3 copy.25
  100.3 6.0 %all-to-all-start.2 = ((bf16[16,128,256]{1,2,0:T(8,128)(2,1)}), bf16[16,128,256]{1,2,0:T(8,128)(2,1)S(1)}, u32[]{:S(2)}, u32[]{:S(2)}) async-start(bf16[16,128,256]{1,2,0:T(8,128)(2,1)} %copy.25), calls=%async_computation.2 | async-start | bytes 2097152 | tf_op jit(solution)/shard_map/all_to_all | solution.py:102
  106.3 0.1 eq.25
  106.5 0.1 eq.29
  106.9 0.6 reduce-window.6
  107.5 0.2 slice_reduce_fusion
  107.8 42.2 %all-to-all-done.2 = bf16[16,128,256]{1,2,0:T(8,128)(2,1)S(1)} async-done(((bf16[16,128,256]{1,2,0:T(8,128)(2,1)}), bf16[16,128,256]{1,2,0:T(8,128)(2,1)S(1)}, u32[]{:S(2)}, u32[]{:S(2)}) %all-to-all-start.2) | async-done | bytes 1048608 | tf_op jit(solution)/shard_map/all_to_all | solution.py:102
  150.0 76.5 %all-gather.6.cloned.1.call-done = bf16[16,256,2048]{2,1,0:T(8,128)(2,1)} async-done(((bf16[16,16,2048]{2,1,0:T(8,128)(2,1)}), bf16[16,256,2048]{2,1,0:T(8,128)(2,1)}) %all-gather.6.cloned.1.call-update) | async-done | bytes 16777232 | tf_op jit(solution)/shard_map/all_gather | solution.py:111
  226.5 8.6 %multiply_reduce_fusion.1 = (f32[128]{0:T(128)S(1)}, f32[128,2048]{1,0:T(8,128)S(1)}) fusion(bf16[128,4096]{0,1:T(8,128)(2,1)} %bitcast.86, bf16[4096,2048]{1,0:T(8,128)(2,1)} %bitcast.84, bf16[128,1,2048]{2,0,1:T(8,128)(2,1)} %param.13), kind=kOutput, calls=%fused_computation.16 | convolution fusion | flops 2148532224 | bytes 19399168 | tf_op jit(solution)/shard_map/dot_general | solution.py:112
  235.1 0.2 multiply_convert_fusion
  235.2 1.6 broadcast_in_dim.5
  236.8 2.3 reshape.158
  239.1 4.4 %scatter_custom_fusion = bf16[512,2048]{1,0:T(8,128)(2,1)} fusion(s32[256]{0:T(256)S(1)} %bitcast.92, bf16[256,2048]{1,0:T(8,128)(2,1)} %reshape.158, bf16[]{:T(256)} %constant.8.clone.1), kind=kCustom, calls=%fused_computation.17 | custom fusion | bytes 2097664 | tf_op jit(solution)/shard_map/scatter | solution.py:130
  243.5 54.1 %all_to_all.34 = bf16[16,1,32,2048]{3,2,1,0:T(8,128)(2,1)S(1)} all-to-all(bf16[16,1,32,2048]{3,2,1,0:T(8,128)(2,1)} %bitcast.85), channel_id=1, replica_groups=mesh['grp'=2,'head'=16] {'head'}, dimensions={0} | all-to-all | bytes 4194304 | tf_op jit(solution)/shard_map/all_to_all | solution.py:135
  297.6 2.3 fusion.5
  300.0 2.6 fusion.2
  302.6 4.9 %all-to-all-start.4 = ((bf16[1,16,32,2048]{3,2,0,1:T(8,128)(2,1)}), bf16[1,16,32,2048]{3,2,0,1:T(8,128)(2,1)}, u32[]{:S(2)}, u32[]{:S(2)}) async-start(bf16[1,16,32,2048]{3,2,0,1:T(8,128)(2,1)} %fusion.2), calls=%async_computation.4 | async-start | bytes 4194304 | tf_op jit(solution)/shard_map/all_to_all | solution.py:145
  307.6 47.4 %all-to-all-done.4 = bf16[1,16,32,2048]{3,2,0,1:T(8,128)(2,1)} async-done(((bf16[1,16,32,2048]{3,2,0,1:T(8,128)(2,1)}), bf16[1,16,32,2048]{3,2,0,1:T(8,128)(2,1)}, u32[]{:S(2)}, u32[]{:S(2)}) %all-to-all-start.4) | async-done | bytes 2097184 | tf_op jit(solution)/shard_map/all_to_all | solution.py:145
  355.0 5.2 %gather_fusion = bf16[256,2048]{1,0:T(8,128)(2,1)} fusion(bf16[512,2048]{1,0:T(8,128)(2,1)} %bitcast.28, s32[1024]{0:T(1024)S(1)} %pad_clamp_fusion), kind=kCustom, calls=%fused_computation | custom fusion | bytes 2098176 | tf_op jit(solution)/shard_map/gather | solution.py:146
  360.2 3.4 reshape.145
  363.6 4.8 %multiply_reduce_fusion = f32[128,2048]{1,0:T(8,128)S(1)} fusion(f32[128,2,2048]{2,1,0:T(2,128)} %reshape.145, f32[128,2]{1,0:T(8,128)S(1)} %copy.31), kind=kLoop, calls=%fused_computation.9 | loop fusion | flops 786432 | bytes 3146752 | tf_op jit(solution)/shard_map/reduce_sum | solution.py:148
  368.4 0.9 fusion.13
  (33 shorter events, 0.8 us)
Async XLA Ops:
  6.5 293.4 %copy-start = (bf16[1,512,2048]{2,1,0:T(8,128)(2,1)S(1)}, bf16[1,512,2048]{2,1,0:T(8,128)(2,1)}, u32[]{:S(2)}) copy-start(bf16[1,512,2048]{2,1,0:T(8,128)(2,1)} %param.19) | copy-start | bytes 6291460
  6.5 12.2 %copy-start.2 = (bf16[128,1,16,256]{3,2,1,0:T(8,128)(2,1)S(1)}, bf16[128,1,16,256]{3,2,1,0:T(8,128)(2,1)}, u32[]{:S(2)}) copy-start(bf16[128,1,16,256]{3,2,1,0:T(8,128)(2,1)} %param.10) | copy-start | bytes 3145732
  6.5 48.2 %all-gather.10.cloned.1.call-start = ((), (), s32[]{:S(2)}) async-start(), calls=%async_computation.7 | async-start | bytes 2359296 | tf_op jit(solution)/shard_map/all_gather | solution.py:98
  17.2 61.7 %all-gather.8.cloned.1.call-start = ((), (), s32[]{:S(2)}) async-start(), calls=%async_computation.6 | async-start | bytes 2359296 | tf_op jit(solution)/shard_map/all_gather | solution.py:97
  18.0 208.5 %all-gather.6.cloned.1.call-start = ((), (), s32[]{:S(2)}) async-start(), calls=%async_computation.5 | async-start | bytes 17825792 | tf_op jit(solution)/shard_map/all_gather | solution.py:111
  20.0 37.8 %all-to-all-start = ((bf16[16,128,256]{2,1,0:T(8,128)(2,1)}), bf16[16,128,256]{2,1,0:T(8,128)(2,1)S(1)}, u32[]{:S(2)}, u32[]{:S(2)}) async-start(bf16[16,128,256]{2,1,0:T(8,128)(2,1)} %bitcast.82), calls=%async_computation | async-start | bytes 2097152 | tf_op jit(solution)/shard_map/all_to_all | solution.py:100
  57.8 21.1 %copy-start.3 = (bf16[16,128,256]{2,1,0:T(8,128)(2,1)}, bf16[16,128,256]{2,1,0:T(8,128)(2,1)S(1)}, u32[]{:S(2)}) copy-start(bf16[16,128,256]{2,1,0:T(8,128)(2,1)S(1)} %all-to-all-done) | copy-start | bytes 3145732
  98.0 8.2 %copy-start.5 = (s32[128,1,2]{0,2,1:T(2,128)S(1)}, s32[128,1,2]{0,2,1:T(2,128)}, u32[]{:S(2)}) copy-start(s32[128,1,2]{0,2,1:T(2,128)} %param.16) | copy-start | bytes 3076
  100.3 49.7 %all-to-all-start.2 = ((bf16[16,128,256]{1,2,0:T(8,128)(2,1)}), bf16[16,128,256]{1,2,0:T(8,128)(2,1)S(1)}, u32[]{:S(2)}, u32[]{:S(2)}) async-start(bf16[16,128,256]{1,2,0:T(8,128)(2,1)} %copy.25), calls=%async_computation.2 | async-start | bytes 2097152 | tf_op jit(solution)/shard_map/all_to_all | solution.py:102
  150.0 76.5 %copy-start.1 = (bf16[16,128,256]{1,2,0:T(8,128)(2,1)}, bf16[16,128,256]{1,2,0:T(8,128)(2,1)S(1)}, u32[]{:S(2)}) copy-start(bf16[16,128,256]{1,2,0:T(8,128)(2,1)S(1)} %all-to-all-done.2) | copy-start | bytes 3145732
  226.5 8.6 %copy-start.4 = (f32[2048]{0:T(1024)S(1)}, f32[2048]{0:T(1024)}, u32[]{:S(2)}) copy-start(f32[2048]{0:T(1024)} %param.15) | copy-start | bytes 24580
  243.5 54.1 %copy-start.7 = (bf16[1,2048,1024]{2,1,0:T(8,128)(2,1)S(1)}, bf16[1,2048,1024]{2,1,0:T(8,128)(2,1)}, u32[]{:S(2)}) copy-start(bf16[1,2048,1024]{2,1,0:T(8,128)(2,1)} %param.18) | copy-start | bytes 12582916
  302.6 4.9 %copy-start.6 = (f32[128,1,2]{0,2,1:T(2,128)S(1)}, f32[128,1,2]{0,2,1:T(2,128)}, u32[]{:S(2)}) copy-start(f32[128,1,2]{0,2,1:T(2,128)} %param.17) | copy-start | bytes 3076
  302.6 52.5 %all-to-all-start.4 = ((bf16[1,16,32,2048]{3,2,0,1:T(8,128)(2,1)}), bf16[1,16,32,2048]{3,2,0,1:T(8,128)(2,1)}, u32[]{:S(2)}, u32[]{:S(2)}) async-start(bf16[1,16,32,2048]{3,2,0,1:T(8,128)(2,1)} %fusion.2), calls=%async_computation.4 | async-start | bytes 4194304 | tf_op jit(solution)/shard_map/all_to_all | solution.py:145
Sparse Core Ops, SparseCore 0:
  17.3 37.3 all-gather.9
  56.3 22.5 all-gather.7
  81.1 145.3 all-gather.5

commit v2 on v1

--- a/solution.py
+++ b/solution.py
@@ -9,7 +9,12 @@
 eps_norm = 1e-06
 
 
-def attend_kernel(query_ref, cache_ref, new_ref, out_ref, *, block, old_block):
+def swap_in_pair(value):
+    pairs = [(source, source ^ 1) for source in range(lax.axis_size("head"))]
+    return lax.ppermute(value, "head", pairs)
+
+
+def attend_kernel(query_ref, cache_ref, other_ref, new_ref, out_ref, *, block, old_block):
     head_width = query_ref.shape[1]
     step = pl.program_id(0)
     query_rows = query_ref[...] * jnp.asarray(head_width ** (-0.5), query_ref.dtype)
@@ -42,9 +47,10 @@
     carry = fold(
         carry, new_ref[here, :head_width], new_ref[here, head_width:], col_at <= row_at
     )
-    for first in range(0, cache_ref.shape[0], old_block):
-        part = pl.ds(first, old_block)
-        carry = fold(carry, cache_ref[part, :head_width], cache_ref[part, head_width:], None)
+    for old_ref in (cache_ref, other_ref):
+        for first in range(0, old_ref.shape[0], old_block):
+            part = pl.ds(first, old_block)
+            carry = fold(carry, old_ref[part, :head_width], old_ref[part, head_width:], None)
 
     def earlier(index, carry):
         part = pl.ds(index * block, block)
@@ -54,7 +60,7 @@
     out_ref[...] = (weighted / total).astype(out_ref.dtype)
 
 
-def attend(queries, new_pairs, cached):
+def attend(queries, new_pairs, cached, cached_other):
     length, head_width = queries.shape
     block = min(512, length)
     old_block = min(1024, cached.shape[0])
@@ -64,16 +70,17 @@
         in_specs=[
             pl.BlockSpec((block, head_width), lambda i: (i, 0)),
             pl.BlockSpec(cached.shape, lambda i: (0, 0)),
+            pl.BlockSpec(cached_other.shape, lambda i: (0, 0)),
             pl.BlockSpec(new_pairs.shape, lambda i: (0, 0)),
         ],
         out_specs=pl.BlockSpec((block, head_width), lambda i: (i, 0)),
         out_shape=jax.ShapeDtypeStruct((length, head_width), jnp.bfloat16),
         cost_estimate=pl.CostEstimate(
-            flops=4 * length * head_width * (length // 2 + cached.shape[0]),
+            flops=4 * length * head_width * (length // 2 + 2 * cached.shape[0]),
             bytes_accessed=8 * length * head_width * 2,
-            transcendentals=length * (length // 2 + cached.shape[0]),
+            transcendentals=length * (length // 2 + 2 * cached.shape[0]),
         ),
-    )(queries, cached, new_pairs)
+    )(queries, cached, cached_other, new_pairs)
 
 
 def local(queries, new_kv, cache, resid, w_out, norm_gain, expert_ids, expert_gates, w_in, w_down):
@@ -88,17 +95,48 @@
     row_count = local_rows * seq_count
     slots = seq_count * pair_heads
     across = [[c * group_size + j for c in range(slots)] for j in range(group_size)]
-    inside = [[c * group_size + j for j in range(group_size)] for c in range(slots)]
+    inside = [
+        [c * group_size + j for j in range(core, group_size, 2)]
+        for c in range(slots)
+        for core in range(2)
+    ]
+    parity = lax.axis_index("head") % 2
     query_slots = queries.reshape(local_rows, axis_count, head_width).transpose(1, 0, 2)
     pair_slots = new_kv.reshape(local_rows, slots, 2 * head_width).transpose(1, 0, 2)
     pair_slots = lax.all_to_all(
         pair_slots, "head", split_axis=0, concat_axis=0, axis_index_groups=across, tiled=True
     )
     cache_rows = lax.all_gather(cache[0], "head", axis=0, axis_index_groups=inside, tiled=True)
+    head_queries = lax.all_to_all(query_slots, "head", split_axis=0, concat_axis=0, tiled=True)
+    same_core = [list(range(core, axis_count, 2)) for core in range(2)]
+    half = model_width // 2
+    own_half = lax.dynamic_slice_in_dim(w_out, parity * half, half, 2)
+    other_half = swap_in_pair(lax.dynamic_slice_in_dim(w_out, (1 - parity) * half, half, 2))
+    w_pair = jnp.concatenate(
+        [
+            jnp.where(parity == 0, own_half, other_half),
+            jnp.where(parity == 0, other_half, own_half),
+        ],
+        1,
+    )
+    pair_slots, head_queries, cache_rows = lax.optimization_barrier(
+        (pair_slots, head_queries, cache_rows)
+    )
     pairs = lax.all_gather(pair_slots, "head", axis=0, axis_index_groups=inside, tiled=False)
-    pairs = pairs.transpose(1, 0, 2, 3).reshape(axis_count * local_rows, 2 * head_width)
-    head_queries = lax.all_to_all(query_slots, "head", split_axis=0, concat_axis=0, tiled=True)
-    attended = attend(head_queries.reshape(-1, head_width), pairs, cache_rows)
+    cache_other = swap_in_pair(cache_rows)
+    pairs, w_pair = lax.optimization_barrier((pairs, w_pair))
+    w_half = lax.all_gather(w_pair, "head", axis=1, axis_index_groups=same_core, tiled=True)
+    w_half = w_half.reshape(head_count * head_width, half)
+    pairs_other = swap_in_pair(pairs)
+    pairs = jnp.stack(
+        [
+            jnp.where(parity == 0, pairs, pairs_other),
+            jnp.where(parity == 0, pairs_other, pairs),
+        ],
+        1,
+    )
+    pairs = pairs.transpose(2, 0, 1, 3, 4).reshape(axis_count * local_rows, 2 * head_width)
+    attended = attend(head_queries.reshape(-1, head_width), pairs, cache_rows, cache_other)
     returned = lax.all_to_all(
         attended.reshape(axis_count, local_rows, head_width),
         "head",
@@ -108,11 +146,16 @@
     )
     attn_rows = returned.reshape(seq_count, head_count, local_rows, head_width)
     attn_rows = attn_rows.transpose(2, 0, 1, 3).reshape(row_count, head_count * head_width)
-    w_full = lax.all_gather(w_out, "head", axis=1, tiled=True)
-    projected = jnp.dot(
-        attn_rows,
-        w_full.reshape(head_count * head_width, model_width),
-        preferred_element_type=jnp.float32,
+    partner_rows = swap_in_pair(attn_rows)
+    partner_part = jnp.dot(partner_rows, w_half, preferred_element_type=jnp.float32)
+    far_part = swap_in_pair(partner_part)
+    near_part = jnp.dot(attn_rows, w_half, preferred_element_type=jnp.float32)
+    projected = jnp.concatenate(
+        [
+            jnp.where(parity == 0, near_part, far_part),
+            jnp.where(parity == 0, far_part, near_part),
+        ],
+        1,
     )
     stream = resid.reshape(row_count, model_width).astype(jnp.float32) + projected
     normed = stream * lax.rsqrt(jnp.mean(stream * stream, 1, keepdims=True) + eps_norm) * norm_gain
@@ -126,13 +169,24 @@
     earlier = jnp.cumsum(onehot, 0) - onehot
     slot_rank = jnp.sum(earlier * onehot, 1)
     target = flat_ids * capacity + slot_rank
-    repeated = jnp.repeat(normed, top_count, axis=0)
-    outgoing = jnp.zeros((experts * capacity, model_width), jnp.bfloat16).at[target].set(repeated)
-    outgoing = outgoing.reshape(experts, 1, capacity, model_width)
+    target = target.reshape(row_count, top_count)
+    places = jnp.arange(experts * capacity, dtype=jnp.int32)
+    chosen = jnp.zeros((experts * capacity, row_count), jnp.bool_)
+    gate_of = jnp.zeros((row_count, experts * capacity), jnp.float32)
+    gates = expert_gates.reshape(row_count, top_count)
+    for rank in range(top_count):
+        chosen = chosen | (places[:, None] == target[None, :, rank])
+        gate_of = jnp.where(
+            target[:, rank, None] == places[None, :], gates[:, rank, None], gate_of
+        )
+    outgoing = jnp.dot(
+        chosen.astype(jnp.bfloat16), normed, preferred_element_type=jnp.float32
+    ).astype(jnp.bfloat16)
+    outgoing = outgoing.reshape(axis_count, local_experts, capacity, model_width)
     hidden_width = w_down.shape[1]
     inner_act = jnp.einsum(
-        "esmd,edf->esmf",
-        lax.all_to_all(outgoing, "head", split_axis=0, concat_axis=1, tiled=True),
+        "semd,edf->semf",
+        lax.all_to_all(outgoing, "head", split_axis=0, concat_axis=0, tiled=True),
         w_in,
         preferred_element_type=jnp.float32,
     )
@@ -140,12 +194,18 @@
         jnp.bfloat16
     )
     answered = jnp.einsum(
-        "esmf,efd->esmd", hidden, w_down, preferred_element_type=jnp.float32
+        "semf,efd->semd", hidden, w_down, preferred_element_type=jnp.float32
     ).astype(jnp.bfloat16)
-    returned_rows = lax.all_to_all(answered, "head", split_axis=1, concat_axis=0, tiled=True)
-    picked = returned_rows.reshape(experts * capacity, model_width)[target].astype(jnp.float32)
-    weighted = picked * expert_gates.reshape(-1)[:, None]
-    expert_sum = weighted.reshape(row_count, top_count, model_width).sum(1)
+    returned_rows = lax.all_to_all(answered, "head", split_axis=0, concat_axis=0, tiled=True)
+    picked = returned_rows.reshape(experts * capacity, model_width)
+    expert_sum = jnp.zeros((row_count, model_width), jnp.float32)
+    rest = gate_of
+    for _ in range(3):
+        term = lax.reduce_precision(rest, 8, 7)
+        rest = rest - term
+        expert_sum = expert_sum + jnp.dot(
+            term.astype(jnp.bfloat16), picked, preferred_element_type=jnp.float32
+        )
     return (stream + expert_sum).astype(jnp.bfloat16).reshape(local_rows, seq_count, model_width)
 
 

time: 376 us -> 366 us (0.973)
  waiting for transfers between devices: 216 us -> 178 us
  blocking collectives: 63.6 us -> 96.9 us
  local copies, waits for them, and re-layouts: 25.7 us -> 13.1 us
  matrix products: 13.5 us -> 19.6 us
    all_to_all x2, waiting for transfers between devices: 89.6 us -> 51.2 us  [the longest x1 47.5 us: local(): lax.all_to_all(answered, 'head', split_axis=0, concat_axis=0, tiled=True)]
    all_to_all x2, blocking collectives: 63.6 us -> 96.9 us  [the longest x1 53.9 us: local(): lax.all_to_all(outgoing, 'head', split_axis=0, concat_axis=0, tiled=True)]
    all_gather x1, waiting for transfers between devices: 21.1 us -> 32.9 us  [local(): lax.all_gather(cache[0], 'head', axis=0, axis_index_groups=inside, tiled=...]
    all_gather x1, waiting for transfers between devices: 76.5 us -> 66.9 us  [local(): lax.all_gather(w_pair, 'head', axis=1, axis_index_groups=same_core, tiled...]
    dot_general x3 -> x8, matrix products: 13.5 us -> 19.6 us  [the longest x3 7.31 us: local(): jnp.dot(term.astype(jnp.bfloat16), picked, preferred_element_type=jnp.flo...]
    all_gather x1, waiting for transfers between devices: 27.4 us -> 21.4 us  [local(): lax.all_gather(pair_slots, 'head', axis=0, axis_index_groups=inside, tile...]
    gather x1 -> x0, local copies, waits for them, and re-layouts: 5.21 us -> none  [local(): returned_rows.reshape(experts * capacity, model_width)[target]]
    ppermute x0 -> x5, waiting for transfers between devices: none -> 4.99 us  [swap_in_pair(): return lax.ppermute(value, 'head', pairs)]
  transfers between devices with their start and end apart: 6 -> 11, of which waited for: 5 -> 9; matrix products, arithmetic and copies ran while one was open for 2% -> 4% of each run, Pallas kernels for 5% -> 5%
where the time goes in v2:
time: 366 us; the launch traced here: 365 us
  waiting for transfers between devices  178 us (49%)
  blocking collectives  96.9 us (26%)
  starting transfers between devices  19.9 us (5%)
  matrix products  19.6 us (5%)
  Pallas kernels  19.1 us (5%)
  between operations  13.3 us (4%)
  local copies, waits for them, and re-layouts  13.1 us (4%)
  other arithmetic  5.28 us (1%)
    all_gather x1, waiting for transfers between devices, local(): lax.all_gather(w_pair, 'head', axis=1, axis_index_groups=same_core, tiled...  66.9 us
    all_to_all x1, blocking collectives, local(): lax.all_to_all(outgoing, 'head', split_axis=0, concat_axis=0, tiled=True)  53.9 us
    all_to_all x1, waiting for transfers between devices, local(): lax.all_to_all(answered, 'head', split_axis=0, concat_axis=0, tiled=True)  47.5 us
    all_to_all x1, blocking collectives, local(): lax.all_to_all(attended.reshape(axis_count, local_rows, head_width), 'hea...  43 us
    all_gather x1, waiting for transfers between devices, local(): lax.all_gather(cache[0], 'head', axis=0, axis_index_groups=inside, tiled=...  32.9 us
    all_gather x1, waiting for transfers between devices, local(): lax.all_gather(pair_slots, 'head', axis=0, axis_index_groups=inside, tile...  21.4 us
    pallas_call x1, Pallas kernels, attend(): pl.pallas_call(functools.partial(attend_kernel, block=block, old_block=ol...  19.1 us
  transfers between devices with their start and end apart: 11, of which 9 were waited for; matrix products, arithmetic and copies ran while one was open for 4% of the time, Pallas kernels for 5%

profile of v2, /device:TPU:13, one launch (start us, length us, event | category | flops | bytes accessed | tf_op | source)
XLA Modules:
  0.0 365.2 jit_solution(15371771472700794169)
XLA Ops:
  6.5 1.8 copy.56
  8.4 3.6 all-to-all-start
  11.9 2.5 copy.55
  14.5 3.7 %all-to-all-done = bf16[2,128,512]{2,1,0:T(8,128)(2,1)S(1)} async-done(((bf16[2,128,512]{2,1,0:T(8,128)(2,1)}), bf16[2,128,512]{2,1,0:T(8,128)(2,1)S(1)}, u32[]{:S(2)}, u32[]{:S(2)}) %all-to-all-start) | async-done | bytes 262176 | tf_op jit(solution)/shard_map/all_to_all | solution.py:106
  18.2 7.1 %all-to-all-start.1 = ((bf16[16,128,256]{2,1,0:T(8,128)(2,1)}), bf16[16,128,256]{2,1,0:T(8,128)(2,1)S(1)}, u32[]{:S(2)}, u32[]{:S(2)}) async-start(bf16[16,128,256]{2,1,0:T(8,128)(2,1)} %bitcast.112), calls=%async_computation.1 | async-start | bytes 2097152 | tf_op jit(solution)/shard_map/all_to_all | solution.py:110
  26.0 32.9 %all-gather.8.cloned.1.call-done = bf16[1,1024,512]{2,1,0:T(8,128)(2,1)} async-done(((bf16[1,256,512]{2,1,0:T(8,128)(2,1)}), bf16[1,1024,512]{2,1,0:T(8,128)(2,1)}) %all-gather.8.cloned.1.call-update) | async-done | bytes 1048592 | tf_op jit(solution)/shard_map/all_gather | solution.py:109
  59.0 2.2 constant_dynamic-slice_fusion
  61.2 1.6 collective-permute-start.1
  62.8 1.9 collective-permute-done.1
  64.7 1.4 broadcast_select_fusion.1
  66.1 1.1 pad_maximum_fusion.1
  67.2 21.4 %all-gather.10.cloned.1.call-done = bf16[8,128,512]{2,1,0:T(8,128)(2,1)} async-done(((bf16[2,128,512]{2,1,0:T(8,128)(2,1)}), bf16[8,128,512]{2,1,0:T(8,128)(2,1)}) %all-gather.10.cloned.1.call-update) | async-done | bytes 1048592 | tf_op jit(solution)/shard_map/all_gather | solution.py:125
  88.7 1.5 copy.39
  90.2 0.8 collective-permute-start.2
  91.0 2.2 collective-permute-done.2
  93.4 1.6 pad_maximum_fusion
  95.0 1.0 copy-done.12
  95.9 19.1 %shard_map.100 = bf16[2048,256]{1,0:T(8,128)(2,1)} custom-call(bf16[2048,256]{1,0:T(8,128)(2,1)} %bitcast.122, bf16[1024,512]{1,0:T(8,128)(2,1)} %bitcast.125, bf16[1024,512]{1,0:T(8,128)(2,1)} %copy-done.12, bf16[2048,512]{1,0:T(8,128)(2,1)} %bitcast.121), custom_call_target="tpu_custom_call" | custom-call | flops 6442450944 | bytes 8388608 | tf_op jit(solution)/shard_map/pallas_call | solution.py:67
  115.0 2.3 copy.42
  117.4 43.0 %all_to_all.25 = bf16[16,128,256]{1,2,0:T(8,128)(2,1)S(1)} all-to-all(bf16[16,128,256]{1,2,0:T(8,128)(2,1)} %copy.42), channel_id=1, replica_groups=mesh['grp'=2,'head'=16] {'head'}, dimensions={0} | all-to-all | bytes 2097152 | tf_op jit(solution)/shard_map/all_to_all | solution.py:140
  163.2 66.9 %all-gather.6.cloned.1.call-done = bf16[16,256,1024]{2,1,0:T(8,128)(2,1)} async-done(((bf16[16,32,1024]{2,1,0:T(8,128)(2,1)}), bf16[16,256,1024]{2,1,0:T(8,128)(2,1)}) %all-gather.6.cloned.1.call-update) | async-done | bytes 8388624 | tf_op jit(solution)/shard_map/all_gather | solution.py:128
  230.1 5.1 %fusion.51 = f32[128,1024]{1,0:T(8,128)S(1)} fusion(bf16[128,4096]{0,1:T(8,128)(2,1)} %collective-permute-done.3, bf16[4096,1024]{1,0:T(8,128)(2,1)} %bitcast.114), kind=kOutput, calls=%fused_computation.83 | convolution fusion | flops 1073741824 | bytes 9961472 | tf_op jit(solution)/shard_map/dot_general | solution.py:150
  235.2 1.3 collective-permute-start.4
  236.4 1.3 fusion.50
  239.9 53.9 %all_to_all.26 = bf16[16,1,32,2048]{3,2,1,0:T(8,128)(2,1)S(1)} all-to-all(bf16[16,1,32,2048]{3,2,1,0:T(8,128)(2,1)S(1)} %bitcast.116), channel_id=1, replica_groups=mesh['grp'=2,'head'=16] {'head'}, dimensions={0} | all-to-all | bytes 4194304 | tf_op jit(solution)/shard_map/all_to_all | solution.py:189
  293.8 2.4 fusion.8
  296.2 2.6 fusion.2
  298.8 5.0 %all-to-all-start.4 = ((bf16[16,1,32,2048]{3,2,1,0:T(8,128)(2,1)}), bf16[16,1,32,2048]{3,2,1,0:T(8,128)(2,1)}, u32[]{:S(2)}, u32[]{:S(2)}) async-start(bf16[16,1,32,2048]{3,2,1,0:T(8,128)(2,1)} %fusion.2), calls=%async_computation.4 | async-start | bytes 4194304 | tf_op jit(solution)/shard_map/all_to_all | solution.py:199
  303.8 47.5 %all-to-all-done.4 = bf16[16,1,32,2048]{3,2,1,0:T(8,128)(2,1)} async-done(((bf16[16,1,32,2048]{3,2,1,0:T(8,128)(2,1)}), bf16[16,1,32,2048]{3,2,1,0:T(8,128)(2,1)}, u32[]{:S(2)}, u32[]{:S(2)}) %all-to-all-start.4) | async-done | bytes 2097184 | tf_op jit(solution)/shard_map/all_to_all | solution.py:199
  351.3 2.1 fusion.23
  353.5 2.2 convolution_add_fusion.1
  355.7 3.0 fusion.5
  (55 shorter events, 6.0 us)
Async XLA Ops:
  6.5 289.7 %copy-start = (bf16[1,512,2048]{2,1,0:T(8,128)(2,1)S(1)}, bf16[1,512,2048]{2,1,0:T(8,128)(2,1)}, u32[]{:S(2)}) copy-start(bf16[1,512,2048]{2,1,0:T(8,128)(2,1)} %param.19) | copy-start | bytes 6291460
  8.4 9.8 %all-to-all-start = ((bf16[2,128,512]{2,1,0:T(8,128)(2,1)}), bf16[2,128,512]{2,1,0:T(8,128)(2,1)S(1)}, u32[]{:S(2)}, u32[]{:S(2)}) async-start(bf16[2,128,512]{2,1,0:T(8,128)(2,1)} %bitcast.113), calls=%async_computation | async-start | bytes 524288 | tf_op jit(solution)/shard_map/all_to_all | solution.py:106
  18.2 40.7 %copy-start.6 = (bf16[2,128,512]{2,1,0:T(8,128)(2,1)}, bf16[2,128,512]{2,1,0:T(8,128)(2,1)S(1)}, u32[]{:S(2)}) copy-start(bf16[2,128,512]{2,1,0:T(8,128)(2,1)S(1)} %all-to-all-done) | copy-start | bytes 786436
  18.2 40.7 %all-to-all-start.1 = ((bf16[16,128,256]{2,1,0:T(8,128)(2,1)}), bf16[16,128,256]{2,1,0:T(8,128)(2,1)S(1)}, u32[]{:S(2)}, u32[]{:S(2)}) async-start(bf16[16,128,256]{2,1,0:T(8,128)(2,1)} %bitcast.112), calls=%async_computation.1 | async-start | bytes 2097152 | tf_op jit(solution)/shard_map/all_to_all | solution.py:110
  25.3 33.6 %all-gather.8.cloned.1.call-start = ((), (), s32[]{:S(2)}) async-start(), calls=%async_computation.6 | async-start | bytes 1310720 | tf_op jit(solution)/shard_map/all_gather | solution.py:109
  26.0 62.6 %all-gather.10.cloned.1.call-start = ((), (), s32[]{:S(2)}) async-start(), calls=%async_computation.7 | async-start | bytes 1310720 | tf_op jit(solution)/shard_map/all_gather | solution.py:125
  58.9 8.3 %copy-start.5 = (bf16[16,128,256]{2,1,0:T(8,128)(2,1)}, bf16[16,128,256]{2,1,0:T(8,128)(2,1)S(1)}, u32[]{:S(2)}) copy-start(bf16[16,128,256]{2,1,0:T(8,128)(2,1)S(1)} %all-to-all-done.1) | copy-start | bytes 3145732
  58.9 171.1 %all-gather.6.cloned.1.call-start = ((), (), s32[]{:S(2)}) async-start(), calls=%async_computation.5 | async-start | bytes 9437184 | tf_op jit(solution)/shard_map/all_gather | solution.py:128
  61.2 3.5 collective-permute-start.1
  88.6 4.6 %copy-start.4 = (bf16[8,128,512]{2,1,0:T(8,128)(2,1)S(1)}, bf16[8,128,512]{2,1,0:T(8,128)(2,1)}, u32[]{:S(2)}) copy-start(bf16[8,128,512]{2,1,0:T(8,128)(2,1)} %all-gather.10.cloned.1.call-done) | copy-start | bytes 3145732
  88.7 2.3 copy-start.11
  90.2 3.1 collective-permute-start.2
  91.0 4.0 %collective-permute-start = (bf16[1024,512]{1,0:T(8,128)(2,1)S(1)}, bf16[1024,512]{1,0:T(8,128)(2,1)S(1)}, u32[]{:S(2)}, u32[]{:S(2)}) collective-permute-start(bf16[1024,512]{1,0:T(8,128)(2,1)S(1)} %bitcast.126), channel_id=1, source_target_pairs={{0,1},{1,0},{2,3},{3,2},{4,5},{5,4},{6,7},{7,6},{8,9},{9,8},{10,11... | collective-permute-start | bytes 3145736 | tf_op jit(solution)/shard_map/ppermute | solution.py:14
  95.0 1.0 copy-start.12
  115.0 45.7 %copy-start.8 = (s32[128,1,2]{0,2,1:T(2,128)S(1)}, s32[128,1,2]{0,2,1:T(2,128)}, u32[]{:S(2)}) copy-start(s32[128,1,2]{0,2,1:T(2,128)} %param.16) | copy-start | bytes 3076
  160.4 2.8 collective-permute-start.3
  230.1 6.4 %copy-start.1 = (bf16[16,256,1024]{2,1,0:T(8,128)(2,1)S(1)}, bf16[16,256,1024]{2,1,0:T(8,128)(2,1)}, u32[]{:S(2)}) copy-start(bf16[16,256,1024]{2,1,0:T(8,128)(2,1)} %all-gather.6.cloned.1.call-done) | copy-start | bytes 25165828
  235.2 2.8 collective-permute-start.4
  237.8 1.0 copy-start.2
  237.8 1.3 copy-start.7
  239.9 53.9 %copy-start.10 = (bf16[1,2048,1024]{2,1,0:T(8,128)(2,1)S(1)}, bf16[1,2048,1024]{2,1,0:T(8,128)(2,1)}, u32[]{:S(2)}) copy-start(bf16[1,2048,1024]{2,1,0:T(8,128)(2,1)} %param.18) | copy-start | bytes 12582916
  298.8 5.0 %copy-start.9 = (f32[128,1,2]{0,2,1:T(2,128)S(1)}, f32[128,1,2]{0,2,1:T(2,128)}, u32[]{:S(2)}) copy-start(f32[128,1,2]{0,2,1:T(2,128)} %param.17) | copy-start | bytes 3076
  298.8 52.5 %all-to-all-start.4 = ((bf16[16,1,32,2048]{3,2,1,0:T(8,128)(2,1)}), bf16[16,1,32,2048]{3,2,1,0:T(8,128)(2,1)}, u32[]{:S(2)}, u32[]{:S(2)}) async-start(bf16[16,1,32,2048]{3,2,1,0:T(8,128)(2,1)} %fusion.2), calls=%async_computation.4 | async-start | bytes 4194304 | tf_op jit(solution)/shard_map/all_to_all | solution.py:199
  353.4 2.2 copy-start.3
Sparse Core Ops, SparseCore 0:
  27.6 31.2 all-gather.7
  60.4 28.1 all-gather.9
  90.8 139.1 all-gather.5

commit v3 on v2

--- a/solution.py
+++ b/solution.py
@@ -4,19 +4,41 @@
 import jax.numpy as jnp
 from jax import lax
 from jax.experimental import pallas as pl
+from jax.experimental.pallas import tpu as pltpu
 from jax.sharding import PartitionSpec as P
 
 eps_norm = 1e-06
 
 
-def swap_in_pair(value):
-    pairs = [(source, source ^ 1) for source in range(lax.axis_size("head"))]
+def partner_2(value, stride):
+    mask = 2**stride
+    pairs = [(source, source ^ mask) for source in range(lax.axis_size("head"))]
     return lax.ppermute(value, "head", pairs)
 
 
-def attend_kernel(query_ref, cache_ref, other_ref, new_ref, out_ref, *, block, old_block):
+def turn_grp(value, shift):
+    count = lax.axis_size("grp")
+    return lax.ppermute(value, "grp", [(i, (i + shift) % count) for i in range(count)])
+
+
+def attend_kernel(
+    me_ref, query_ref, cache_ref, other_ref, pairs_ref, out_ref, new_ref, *, block, old_block, order
+):
     head_width = query_ref.shape[1]
     step = pl.program_id(0)
+    members, slots, local_rows = pairs_ref.shape[:3]
+
+    @pl.when(step == 0)
+    def _():
+        for slot in range(slots):
+            for member in range(members):
+                apart = member ^ me_ref[0]
+                place = 0
+                for rank, bit in enumerate(order):
+                    place = place + ((apart >> bit) & 1) * 2**rank
+                first = (slot * members + member) * local_rows
+                new_ref[first : first + local_rows, :] = pairs_ref[place, slot]
+
     query_rows = query_ref[...] * jnp.asarray(head_width ** (-0.5), query_ref.dtype)
 
     def fold(carry, keys, values, mask):
@@ -60,27 +82,31 @@
     out_ref[...] = (weighted / total).astype(out_ref.dtype)
 
 
-def attend(queries, new_pairs, cached, cached_other):
+def attend(me, queries, new_pairs, cached, cached_other, order):
     length, head_width = queries.shape
     block = min(512, length)
     old_block = min(1024, cached.shape[0])
     return pl.pallas_call(
-        functools.partial(attend_kernel, block=block, old_block=old_block),
-        grid=(length // block,),
-        in_specs=[
-            pl.BlockSpec((block, head_width), lambda i: (i, 0)),
-            pl.BlockSpec(cached.shape, lambda i: (0, 0)),
-            pl.BlockSpec(cached_other.shape, lambda i: (0, 0)),
-            pl.BlockSpec(new_pairs.shape, lambda i: (0, 0)),
-        ],
-        out_specs=pl.BlockSpec((block, head_width), lambda i: (i, 0)),
+        functools.partial(attend_kernel, block=block, old_block=old_block, order=order),
+        grid_spec=pltpu.PrefetchScalarGridSpec(
+            num_scalar_prefetch=1,
+            grid=(length // block,),
+            in_specs=[
+                pl.BlockSpec((block, head_width), lambda i, me: (i, 0)),
+                pl.BlockSpec(cached.shape, lambda i, me: (0, 0)),
+                pl.BlockSpec(cached_other.shape, lambda i, me: (0, 0)),
+                pl.BlockSpec(new_pairs.shape, lambda i, me: (0, 0, 0, 0)),
+            ],
+            out_specs=pl.BlockSpec((block, head_width), lambda i, me: (i, 0)),
+            scratch_shapes=[pltpu.VMEM((length, 2 * head_width), jnp.bfloat16)],
+        ),
         out_shape=jax.ShapeDtypeStruct((length, head_width), jnp.bfloat16),
         cost_estimate=pl.CostEstimate(
             flops=4 * length * head_width * (length // 2 + 2 * cached.shape[0]),
             bytes_accessed=8 * length * head_width * 2,
             transcendentals=length * (length // 2 + 2 * cached.shape[0]),
         ),
-    )(queries, cached, cached_other, new_pairs)
+    )(me, queries, cached, cached_other, new_pairs)
 
 
 def local(queries, new_kv, cache, resid, w_out, norm_gain, expert_ids, expert_gates, w_in, w_down):
@@ -95,48 +121,31 @@
     row_count = local_rows * seq_count
     slots = seq_count * pair_heads
     across = [[c * group_size + j for c in range(slots)] for j in range(group_size)]
-    inside = [
-        [c * group_size + j for j in range(core, group_size, 2)]
-        for c in range(slots)
-        for core in range(2)
-    ]
-    parity = lax.axis_index("head") % 2
     query_slots = queries.reshape(local_rows, axis_count, head_width).transpose(1, 0, 2)
     pair_slots = new_kv.reshape(local_rows, slots, 2 * head_width).transpose(1, 0, 2)
     pair_slots = lax.all_to_all(
         pair_slots, "head", split_axis=0, concat_axis=0, axis_index_groups=across, tiled=True
     )
-    cache_rows = lax.all_gather(cache[0], "head", axis=0, axis_index_groups=inside, tiled=True)
+    grp_count = lax.axis_size("grp")
+    grp_me = lax.axis_index("grp")
+    part_width = model_width // grp_count
+    w_part = lax.dynamic_slice_in_dim(w_out, grp_me * part_width, part_width, 2)
+    w_part = lax.all_gather(w_part, "head", axis=1, tiled=True)
+    w_part = w_part.reshape(head_count * head_width, part_width)
+    bits = group_size.bit_length() - 1
+    order = tuple(range(1, bits)) + (0,)
+    cache_rows = cache[0]
+    pairs = pair_slots[None]
+    for bit in order[:-1]:
+        cache_rows = jnp.concatenate([cache_rows, partner_2(cache_rows, bit)], 0)
+    cache_other = partner_2(cache_rows, 0)
     head_queries = lax.all_to_all(query_slots, "head", split_axis=0, concat_axis=0, tiled=True)
-    same_core = [list(range(core, axis_count, 2)) for core in range(2)]
-    half = model_width // 2
-    own_half = lax.dynamic_slice_in_dim(w_out, parity * half, half, 2)
-    other_half = swap_in_pair(lax.dynamic_slice_in_dim(w_out, (1 - parity) * half, half, 2))
-    w_pair = jnp.concatenate(
-        [
-            jnp.where(parity == 0, own_half, other_half),
-            jnp.where(parity == 0, other_half, own_half),
-        ],
-        1,
-    )
-    pair_slots, head_queries, cache_rows = lax.optimization_barrier(
-        (pair_slots, head_queries, cache_rows)
-    )
-    pairs = lax.all_gather(pair_slots, "head", axis=0, axis_index_groups=inside, tiled=False)
-    cache_other = swap_in_pair(cache_rows)
-    pairs, w_pair = lax.optimization_barrier((pairs, w_pair))
-    w_half = lax.all_gather(w_pair, "head", axis=1, axis_index_groups=same_core, tiled=True)
-    w_half = w_half.reshape(head_count * head_width, half)
-    pairs_other = swap_in_pair(pairs)
-    pairs = jnp.stack(
-        [
-            jnp.where(parity == 0, pairs, pairs_other),
-            jnp.where(parity == 0, pairs_other, pairs),
-        ],
-        1,
-    )
-    pairs = pairs.transpose(2, 0, 1, 3, 4).reshape(axis_count * local_rows, 2 * head_width)
-    attended = attend(head_queries.reshape(-1, head_width), pairs, cache_rows, cache_other)
+    for bit in order:
+        pairs = jnp.concatenate([pairs, partner_2(pairs, bit)], 0)
+    me = (lax.axis_index("head") % group_size).astype(jnp.int32).reshape(1)
+    attended = attend(
+        me, head_queries.reshape(-1, head_width), pairs, cache_rows, cache_other, order
+    )
     returned = lax.all_to_all(
         attended.reshape(axis_count, local_rows, head_width),
         "head",
@@ -146,17 +155,19 @@
     )
     attn_rows = returned.reshape(seq_count, head_count, local_rows, head_width)
     attn_rows = attn_rows.transpose(2, 0, 1, 3).reshape(row_count, head_count * head_width)
-    partner_rows = swap_in_pair(attn_rows)
-    partner_part = jnp.dot(partner_rows, w_half, preferred_element_type=jnp.float32)
-    far_part = swap_in_pair(partner_part)
-    near_part = jnp.dot(attn_rows, w_half, preferred_element_type=jnp.float32)
-    projected = jnp.concatenate(
-        [
-            jnp.where(parity == 0, near_part, far_part),
-            jnp.where(parity == 0, far_part, near_part),
-        ],
-        1,
-    )
+    parts = []
+    for shift in range(1, grp_count):
+        far_rows = turn_grp(attn_rows, shift)
+        far_part = jnp.dot(far_rows, w_part, preferred_element_type=jnp.float32)
+        parts.append(turn_grp(far_part, -shift))
+    projected = []
+    near_part = jnp.dot(attn_rows, w_part, preferred_element_type=jnp.float32)
+    for column in range(grp_count):
+        piece = near_part
+        for shift in range(1, grp_count):
+            piece = jnp.where((grp_me + shift) % grp_count == column, parts[shift - 1], piece)
+        projected.append(piece)
+    projected = jnp.concatenate(projected, 1)
     stream = resid.reshape(row_count, model_width).astype(jnp.float32) + projected
     normed = stream * lax.rsqrt(jnp.mean(stream * stream, 1, keepdims=True) + eps_norm) * norm_gain
     normed = normed.astype(jnp.bfloat16)

time: 366 us -> 340 us (0.929)
  waiting for transfers between devices: 178 us -> 155 us
  local copies, waits for them, and re-layouts: 13.1 us -> 8.84 us
    all_gather x3 -> x1, waiting for transfers between devices: 121 us -> 0.01 us  [local(): w_part = lax.all_gather(w_part, 'head', axis=1, tiled=True)]
    ppermute x5 -> x8, waiting for transfers between devices: 4.99 us -> 108 us  [the longest x6 75.9 us: partner_2(): return lax.ppermute(value, 'head', pairs)]
    all_to_all x1, blocking collectives: 43 us -> 32 us  [local(): lax.all_to_all(attended.reshape(axis_count, local_rows, head_width), 'hea...]
    all_to_all x0 -> x1, blocking collectives: none -> 9.5 us  [local(): lax.all_to_all(pair_slots, 'head', split_axis=0, concat_axis=0, axis_inde...]
    concatenate x1 -> x5, other arithmetic: 1.07 us -> 7.04 us  [the longest x3 3.99 us: local(): pairs = jnp.concatenate([pairs, partner_2(pairs, bit)], 0)]
    all_to_all x1 -> x0, waiting for transfers between devices: 3.68 us -> none  [local(): lax.all_to_all(pair_slots, 'head', split_axis=0, concat_axis=0, axis_inde...]
  transfers between devices with their start and end apart: 11 -> 11, of which waited for: 9 -> 6; matrix products, arithmetic and copies ran while one was open for 4% -> 5% of each run, Pallas kernels for 5% -> 6%
where the time goes in v3:
time: 340 us; the launch traced here: 339 us
  waiting for transfers between devices  155 us (46%)
  blocking collectives  95.4 us (28%)
  starting transfers between devices  19.5 us (6%)
  matrix products  19.5 us (6%)
  Pallas kernels  19.2 us (6%)
  between operations  13.6 us (4%)
  local copies, waits for them, and re-layouts  8.84 us (3%)
  other arithmetic  8.11 us (2%)
    ppermute x6, waiting for transfers between devices, partner_2(): return lax.ppermute(value, 'head', pairs)  75.9 us
    all_to_all x1, blocking collectives, local(): lax.all_to_all(outgoing, 'head', split_axis=0, concat_axis=0, tiled=True)  53.9 us
    all_to_all x1, waiting for transfers between devices, local(): lax.all_to_all(answered, 'head', split_axis=0, concat_axis=0, tiled=True)  47.5 us
    all_to_all x1, blocking collectives, local(): lax.all_to_all(attended.reshape(axis_count, local_rows, head_width), 'hea...  32 us
    ppermute x2, waiting for transfers between devices, turn_grp(): lax.ppermute(value, 'grp', [(i, (i + shift) % count) for i in range(count)])  31.7 us
    pallas_call x1, Pallas kernels, attend(): pl.pallas_call(functools.partial(attend_kernel, block=block, old_block=ol...  19.2 us
    all_to_all x1, blocking collectives, local(): lax.all_to_all(pair_slots, 'head', split_axis=0, concat_axis=0, axis_inde...  9.5 us
    all_to_all x1, starting transfers between devices, local(): lax.all_to_all(query_slots, 'head', split_axis=0, concat_axis=0, tiled=True)  8.41 us
  transfers between devices with their start and end apart: 11, of which 6 were waited for; matrix products, arithmetic and copies ran while one was open for 5% of the time, Pallas kernels for 6%

profile of v3, /device:TPU:13, one launch (start us, length us, event | category | flops | bytes accessed | tf_op | source)
XLA Modules:
  0.0 339.3 jit_solution(15623178876916345346)
XLA Ops:
  6.5 2.0 constant_dynamic-slice_fusion
  8.6 1.0 copy.41
  9.6 9.5 %all_to_all.25 = bf16[2,128,512]{2,1,0:T(8,128)(2,1)S(1)} all-to-all(bf16[2,128,512]{2,1,0:T(8,128)(2,1)S(1)} %bitcast.116), channel_id=1, replica_groups={{0,8},{1,9},{2,10},{3,11},{4,12},{5,13},{6,14},{7,15},{16,24},{17,25},{..., dimensions={0} | all-to-all | bytes 524288 | tf_op jit(solution)/shard_map/all_to_all | solution.py:126
  19.3 1.2 collective-permute-start
  20.6 2.6 copy.40
  23.1 8.4 %all-to-all-start = ((bf16[16,128,256]{2,1,0:T(8,128)(2,1)}), bf16[16,128,256]{2,1,0:T(8,128)(2,1)}, u32[]{:S(2)}, u32[]{:S(2)}) async-start(bf16[16,128,256]{2,1,0:T(8,128)(2,1)} %bitcast.104), calls=%async_computation | async-start | bytes 2097152 | tf_op jit(solution)/shard_map/all_to_all | solution.py:142
  31.9 6.7 %collective-permute-done = bf16[256,512]{1,0:T(8,128)(2,1)} collective-permute-done((bf16[256,512]{1,0:T(8,128)(2,1)S(1)}, bf16[256,512]{1,0:T(8,128)(2,1)}, u32[]{:S(2)}, u32[]{:S(2)}) %collective-permute-start) | collective-permute-done | bytes 262176 | tf_op jit(solution)/shard_map/ppermute | solution.py:16
  38.6 1.0 pad_maximum_fusion.3
  39.7 40.3 %collective-permute-done.4 = bf16[2,2,128,512]{3,2,1,0:T(8,128)(2,1)S(1)} collective-permute-done((bf16[2,2,128,512]{3,2,1,0:T(8,128)(2,1)S(1)}, bf16[2,2,128,512]{3,2,1,0:T(8,128)(2,1)S(1)}, u32[]{:S(2)}, u32[]{:S(2)}) %collective-permute-start.4) | collective-permute-done | bytes 524320 | tf_op jit(solution)/shard_map/ppermute | solution.py:16
  80.0 1.2 pad_maximum_fusion.2
  81.1 0.9 collective-permute-start.5
  82.0 28.9 %collective-permute-done.1 = bf16[512,512]{1,0:T(8,128)(2,1)S(1)} collective-permute-done((bf16[512,512]{1,0:T(8,128)(2,1)S(1)}, bf16[512,512]{1,0:T(8,128)(2,1)S(1)}, u32[]{:S(2)}, u32[]{:S(2)}) %collective-permute-start.1) | collective-permute-done | bytes 524320 | tf_op jit(solution)/shard_map/ppermute | solution.py:16
  110.9 2.1 pad_maximum_fusion.1.cache_ref
  113.6 2.8 pad_maximum_fusion.pairs_ref
  116.4 19.2 %shard_map.100 = bf16[2048,256]{1,0:T(8,128)(2,1)} custom-call(s32[1]{0:T(128)} %bitcast.1.me_ref, bf16[2048,256]{1,0:T(8,128)(2,1)} %bitcast.4.query_ref, bf16[1024,512]{1,0:T(8,128)(2,1)} %pad_maximum_fusion.1.cache_ref, bf16[1024,512]{1,0:T(8,128)(2,1)} %collective-permute-done.2.other_ref, bf16[8,2,128,512]{3,2,1,0:T(8,128)(2,1)} %pad_maximum_fusion.pairs_ref), custom_call_target="tpu_custom_call" | custom-call | flops 6442450944 | bytes 8388608 | tf_op jit(solution)/shard_map/pallas_call | solution.py:89
  135.6 2.3 copy.29
  137.9 32.0 %all_to_all.26 = bf16[16,128,256]{1,2,0:T(8,128)(2,1)S(1)} all-to-all(bf16[16,128,256]{1,2,0:T(8,128)(2,1)} %copy.29), channel_id=1, replica_groups=mesh['grp'=2,'head'=16] {'head'}, dimensions={0} | all-to-all | bytes 2097152 | tf_op jit(solution)/shard_map/all_to_all | solution.py:149
  170.0 1.2 collective-permute-start.6
  172.8 21.8 %collective-permute-done.6 = bf16[128,4096]{0,1:T(8,128)(2,1)} collective-permute-done((bf16[128,4096]{0,1:T(8,128)(2,1)S(1)}, bf16[128,4096]{0,1:T(8,128)(2,1)}, u32[]{:S(2)}, u32[]{:S(2)}) %collective-permute-start.6) | collective-permute-done | bytes 1048608 | tf_op jit(solution)/shard_map/ppermute | solution.py:21
  194.7 5.1 %fusion.50 = f32[128,1024]{1,0:T(8,128)S(1)} fusion(bf16[128,4096]{0,1:T(8,128)(2,1)} %collective-permute-done.6, bf16[4096,1024]{1,0:T(8,128)(2,1)} %bitcast.106), kind=kOutput, calls=%fused_computation.81 | convolution fusion | flops 1073741824 | bytes 9961472 | tf_op jit(solution)/shard_map/dot_general | solution.py:161
  199.8 1.3 collective-permute-start.7
  201.1 1.3 fusion.51
  202.5 9.9 %collective-permute-done.7 = f32[128,1024]{1,0:T(8,128)S(1)} collective-permute-done((f32[128,1024]{1,0:T(8,128)S(1)}, f32[128,1024]{1,0:T(8,128)S(1)}, u32[]{:S(2)}, u32[]{:S(2)}) %collective-permute-start.7) | collective-permute-done | bytes 524320 | tf_op jit(solution)/shard_map/ppermute | solution.py:21
  212.7 0.8 convolution_convert_fusion.1
  213.6 53.9 %all_to_all.27 = bf16[16,1,32,2048]{3,2,1,0:T(8,128)(2,1)S(1)} all-to-all(bf16[16,1,32,2048]{3,2,1,0:T(8,128)(2,1)S(1)} %bitcast.108), channel_id=1, replica_groups=mesh['grp'=2,'head'=16] {'head'}, dimensions={0} | all-to-all | bytes 4194304 | tf_op jit(solution)/shard_map/all_to_all | solution.py:200
  267.4 2.4 fusion.8
  269.8 2.6 fusion.2
  272.4 5.2 %all-to-all-start.4 = ((bf16[16,1,32,2048]{3,2,1,0:T(8,128)(2,1)}), bf16[16,1,32,2048]{3,2,1,0:T(8,128)(2,1)}, u32[]{:S(2)}, u32[]{:S(2)}) async-start(bf16[16,1,32,2048]{3,2,1,0:T(8,128)(2,1)} %fusion.2), calls=%async_computation.4 | async-start | bytes 4194304 | tf_op jit(solution)/shard_map/all_to_all | solution.py:210
  277.6 47.5 %all-to-all-done.4 = bf16[16,1,32,2048]{3,2,1,0:T(8,128)(2,1)} async-done(((bf16[16,1,32,2048]{3,2,1,0:T(8,128)(2,1)}), bf16[16,1,32,2048]{3,2,1,0:T(8,128)(2,1)}, u32[]{:S(2)}, u32[]{:S(2)}) %all-to-all-start.4) | async-done | bytes 2097184 | tf_op jit(solution)/shard_map/all_to_all | solution.py:210
  325.1 2.1 fusion.23
  327.2 2.2 convolution_add_fusion.1
  329.4 3.0 fusion.5
  (46 shorter events, 3.4 us)
Async XLA Ops:
  6.5 263.3 %copy-start = (bf16[1,512,2048]{2,1,0:T(8,128)(2,1)S(1)}, bf16[1,512,2048]{2,1,0:T(8,128)(2,1)}, u32[]{:S(2)}) copy-start(bf16[1,512,2048]{2,1,0:T(8,128)(2,1)} %param.19) | copy-start | bytes 6291460
  6.5 12.8 %copy-start.4 = (bf16[1,256,512]{2,1,0:T(8,128)(2,1)S(1)}, bf16[1,256,512]{2,1,0:T(8,128)(2,1)}, u32[]{:S(2)}) copy-start(bf16[1,256,512]{2,1,0:T(8,128)(2,1)} %param.12) | copy-start | bytes 786436
  6.5 188.1 %all-gather.2.cloned.1.call-start = ((), (), s32[]{:S(2)}) async-start(), calls=%async_computation.5 | async-start | bytes 8912896 | tf_op jit(solution)/shard_map/all_gather | solution.py:133
  19.1 12.4 %collective-permute-start.3 = (bf16[1,2,128,512]{3,2,1,0:T(8,128)(2,1)S(1)}, bf16[1,2,128,512]{3,2,1,0:T(8,128)(2,1)S(1)}, u32[]{:S(2)}, u32[]{:S(2)}) collective-permute-start(bf16[1,2,128,512]{3,2,1,0:T(8,128)(2,1)S(1)} %bitcast.111), channel_id=1, source_target_pairs={{0,2},{1,3},{2,0},{3,1},{4,6},{5,7},{6,4},{7,5},{8,10},{9,11},{10,... | collective-permute-start | bytes 786440 | tf_op jit(solution)/shard_map/ppermute | solution.py:16
  19.3 19.3 %collective-permute-start = (bf16[256,512]{1,0:T(8,128)(2,1)S(1)}, bf16[256,512]{1,0:T(8,128)(2,1)}, u32[]{:S(2)}, u32[]{:S(2)}) collective-permute-start(bf16[256,512]{1,0:T(8,128)(2,1)S(1)} %bitcast.117), channel_id=1, source_target_pairs={{0,2},{1,3},{2,0},{3,1},{4,6},{5,7},{6,4},{7,5},{8,10},{9,11},{10,... | collective-permute-start | bytes 786440 | tf_op jit(solution)/shard_map/ppermute | solution.py:16
  23.1 93.3 %all-to-all-start = ((bf16[16,128,256]{2,1,0:T(8,128)(2,1)}), bf16[16,128,256]{2,1,0:T(8,128)(2,1)}, u32[]{:S(2)}, u32[]{:S(2)}) async-start(bf16[16,128,256]{2,1,0:T(8,128)(2,1)} %bitcast.104), calls=%async_computation | async-start | bytes 2097152 | tf_op jit(solution)/shard_map/all_to_all | solution.py:142
  31.6 48.4 %collective-permute-start.4 = (bf16[2,2,128,512]{3,2,1,0:T(8,128)(2,1)S(1)}, bf16[2,2,128,512]{3,2,1,0:T(8,128)(2,1)S(1)}, u32[]{:S(2)}, u32[]{:S(2)}) collective-permute-start(bf16[2,2,128,512]{3,2,1,0:T(8,128)(2,1)S(1)} %pad_maximum_fusion.4), channel_id=1, source_target_pairs={{0,4},{1,5},{2,6},{3,7},{4,0},{5,1},{6,2},{7,3},{8,12},{9,13},{10,... | collective-permute-start | bytes 1572872 | tf_op jit(solution)/shard_map/ppermute | solution.py:16
  39.6 71.2 %collective-permute-start.1 = (bf16[512,512]{1,0:T(8,128)(2,1)S(1)}, bf16[512,512]{1,0:T(8,128)(2,1)S(1)}, u32[]{:S(2)}, u32[]{:S(2)}) collective-permute-start(bf16[512,512]{1,0:T(8,128)(2,1)S(1)} %pad_maximum_fusion.3), channel_id=1, source_target_pairs={{0,4},{1,5},{2,6},{3,7},{4,0},{5,1},{6,2},{7,3},{8,12},{9,13},{10,... | collective-permute-start | bytes 1572872 | tf_op jit(solution)/shard_map/ppermute | solution.py:16
  81.1 32.5 %collective-permute-start.5 = (bf16[4,2,128,512]{3,2,1,0:T(8,128)(2,1)}, bf16[4,2,128,512]{3,2,1,0:T(8,128)(2,1)}, u32[]{:S(2)}, u32[]{:S(2)}) collective-permute-start(bf16[4,2,128,512]{3,2,1,0:T(8,128)(2,1)} %pad_maximum_fusion.2), channel_id=1, source_target_pairs={{0,1},{1,0},{2,3},{3,2},{4,5},{5,4},{6,7},{7,6},{8,9},{9,8},{10,11... | collective-permute-start | bytes 3145736 | tf_op jit(solution)/shard_map/ppermute | solution.py:16
  112.9 3.5 %collective-permute-start.2 = (bf16[1024,512]{1,0:T(8,128)(2,1)}, bf16[1024,512]{1,0:T(8,128)(2,1)}, u32[]{:S(2)}, u32[]{:S(2)}) collective-permute-start(bf16[1024,512]{1,0:T(8,128)(2,1)} %pad_maximum_fusion.1.cache_ref), channel_id=1, source_target_pairs={{0,1},{1,0},{2,3},{3,2},{4,5},{5,4},{6,7},{7,6},{8,9},{9,8},{10,11... | collective-permute-start | bytes 3145736 | tf_op jit(solution)/shard_map/ppermute | solution.py:16
  135.6 35.6 %copy-start.6 = (s32[128,1,2]{0,2,1:T(2,128)S(1)}, s32[128,1,2]{0,2,1:T(2,128)}, u32[]{:S(2)}) copy-start(s32[128,1,2]{0,2,1:T(2,128)} %param.16) | copy-start | bytes 3076
  170.0 24.7 %collective-permute-start.6 = (bf16[128,4096]{0,1:T(8,128)(2,1)S(1)}, bf16[128,4096]{0,1:T(8,128)(2,1)}, u32[]{:S(2)}, u32[]{:S(2)}) collective-permute-start(bf16[128,4096]{0,1:T(8,128)(2,1)S(1)} %bitcast.109), channel_id=1, source_target_pairs={{0,16},{16,0},{1,17},{17,1},{2,18},{18,2},{3,19},{19,3},{4,20},{20... | collective-permute-start | bytes 3145736 | tf_op jit(solution)/shard_map/ppermute | solution.py:21
  194.7 6.4 %copy-start.1 = (bf16[16,256,1024]{2,1,0:T(8,128)(2,1)S(1)}, bf16[16,256,1024]{2,1,0:T(8,128)(2,1)}, u32[]{:S(2)}) copy-start(bf16[16,256,1024]{2,1,0:T(8,128)(2,1)} %all-gather.2.cloned.1.call-done) | copy-start | bytes 25165828
  199.8 12.6 %collective-permute-start.7 = (f32[128,1024]{1,0:T(8,128)S(1)}, f32[128,1024]{1,0:T(8,128)S(1)}, u32[]{:S(2)}, u32[]{:S(2)}) collective-permute-start(f32[128,1024]{1,0:T(8,128)S(1)} %fusion.50), channel_id=1, source_target_pairs={{0,16},{16,0},{1,17},{17,1},{2,18},{18,2},{3,19},{19,3},{4,20},{20... | collective-permute-start | bytes 1572872 | tf_op jit(solution)/shard_map/ppermute | solution.py:21
  202.4 10.0 %copy-start.2 = (bf16[128,1,2048]{2,0,1:T(8,128)(2,1)S(1)}, bf16[128,1,2048]{2,0,1:T(8,128)(2,1)}, u32[]{:S(2)}) copy-start(bf16[128,1,2048]{2,0,1:T(8,128)(2,1)} %param.13) | copy-start | bytes 1572868
  202.4 10.3 %copy-start.5 = (f32[2048]{0:T(1024)S(1)}, f32[2048]{0:T(1024)}, u32[]{:S(2)}) copy-start(f32[2048]{0:T(1024)} %param.15) | copy-start | bytes 24580
  213.5 53.9 %copy-start.8 = (bf16[1,2048,1024]{2,1,0:T(8,128)(2,1)S(1)}, bf16[1,2048,1024]{2,1,0:T(8,128)(2,1)}, u32[]{:S(2)}) copy-start(bf16[1,2048,1024]{2,1,0:T(8,128)(2,1)} %param.18) | copy-start | bytes 12582916
  272.4 5.2 %copy-start.7 = (f32[128,1,2]{0,2,1:T(2,128)S(1)}, f32[128,1,2]{0,2,1:T(2,128)}, u32[]{:S(2)}) copy-start(f32[128,1,2]{0,2,1:T(2,128)} %param.17) | copy-start | bytes 3076
  272.4 52.7 %all-to-all-start.4 = ((bf16[16,1,32,2048]{3,2,1,0:T(8,128)(2,1)}), bf16[16,1,32,2048]{3,2,1,0:T(8,128)(2,1)}, u32[]{:S(2)}, u32[]{:S(2)}) async-start(bf16[16,1,32,2048]{3,2,1,0:T(8,128)(2,1)} %fusion.2), calls=%async_computation.4 | async-start | bytes 4194304 | tf_op jit(solution)/shard_map/all_to_all | solution.py:210
  327.2 2.2 copy-start.3
Sparse Core Ops, SparseCore 0:
  9.5 104.2 all-gather.1

commit v4 on v3

--- a/solution.py
+++ b/solution.py
@@ -130,18 +130,22 @@
     grp_me = lax.axis_index("grp")
     part_width = model_width // grp_count
     w_part = lax.dynamic_slice_in_dim(w_out, grp_me * part_width, part_width, 2)
-    w_part = lax.all_gather(w_part, "head", axis=1, tiled=True)
-    w_part = w_part.reshape(head_count * head_width, part_width)
     bits = group_size.bit_length() - 1
     order = tuple(range(1, bits)) + (0,)
     cache_rows = cache[0]
     pairs = pair_slots[None]
     for bit in order[:-1]:
         cache_rows = jnp.concatenate([cache_rows, partner_2(cache_rows, bit)], 0)
+    head_queries = lax.all_to_all(query_slots, "head", split_axis=0, concat_axis=0, tiled=True)
+    for bit in order[:-1]:
+        pairs = jnp.concatenate([pairs, partner_2(pairs, bit)], 0)
+    w_part, pairs, cache_rows, head_queries = lax.optimization_barrier(
+        (w_part, pairs, cache_rows, head_queries)
+    )
+    w_part = lax.all_gather(w_part, "head", axis=1, tiled=True)
+    w_part = w_part.reshape(head_count * head_width, part_width)
     cache_other = partner_2(cache_rows, 0)
-    head_queries = lax.all_to_all(query_slots, "head", split_axis=0, concat_axis=0, tiled=True)
-    for bit in order:
-        pairs = jnp.concatenate([pairs, partner_2(pairs, bit)], 0)
+    pairs = jnp.concatenate([pairs, partner_2(pairs, 0)], 0)
     me = (lax.axis_index("head") % group_size).astype(jnp.int32).reshape(1)
     attended = attend(
         me, head_queries.reshape(-1, head_width), pairs, cache_rows, cache_other, order
@@ -159,7 +163,7 @@
     for shift in range(1, grp_count):
         far_rows = turn_grp(attn_rows, shift)
         far_part = jnp.dot(far_rows, w_part, preferred_element_type=jnp.float32)
-        parts.append(turn_grp(far_part, -shift))
+        parts.append(turn_grp(far_part.astype(jnp.bfloat16), -shift).astype(jnp.float32))
     projected = []
     near_part = jnp.dot(attn_rows, w_part, preferred_element_type=jnp.float32)
     for column in range(grp_count):

time: 340 us -> 321 us (0.944)
  waiting for transfers between devices: 155 us -> 112 us
  blocking collectives: 95.4 us -> 113 us
  starting transfers between devices: 19.5 us -> 25.2 us
    ppermute x6, waiting for transfers between devices: 75.9 us -> 33.7 us  [partner_2(): return lax.ppermute(value, 'head', pairs)]
    all_to_all x1, blocking collectives: 32 us -> 59.4 us  [local(): lax.all_to_all(attended.reshape(axis_count, local_rows, head_width), 'hea...]
    all_to_all x1 -> x0, blocking collectives: 9.5 us -> none  [local(): lax.all_to_all(pair_slots, 'head', split_axis=0, concat_axis=0, axis_inde...]
    ppermute x2, waiting for transfers between devices: 31.7 us -> 26.7 us  [turn_grp(): lax.ppermute(value, 'grp', [(i, (i + shift) % count) for i in range(count)])]
    all_to_all x0 -> x1, waiting for transfers between devices: none -> 3.65 us  [local(): lax.all_to_all(pair_slots, 'head', split_axis=0, concat_axis=0, axis_inde...]
    all_to_all x0 -> x1, starting transfers between devices: none -> 3.58 us  [local(): lax.all_to_all(pair_slots, 'head', split_axis=0, concat_axis=0, axis_inde...]
  transfers between devices with their start and end apart: 11 -> 12, of which waited for: 6 -> 9; matrix products, arithmetic and copies ran while one was open for 5% -> 5% of each run, Pallas kernels for 6% -> 6%
where the time goes in v4:
time: 321 us; the launch traced here: 320 us
  blocking collectives  113 us (35%)
  waiting for transfers between devices  112 us (35%)
  starting transfers between devices  25.2 us (8%)
  matrix products  19.5 us (6%)
  Pallas kernels  19.2 us (6%)
  between operations  13.6 us (4%)
  local copies, waits for them, and re-layouts  10.3 us (3%)
  other arithmetic  8 us (2%)
    all_to_all x1, blocking collectives, local(): lax.all_to_all(attended.reshape(axis_count, local_rows, head_width), 'hea...  59.4 us
    all_to_all x1, blocking collectives, local(): lax.all_to_all(outgoing, 'head', split_axis=0, concat_axis=0, tiled=True)  53.1 us
    all_to_all x1, waiting for transfers between devices, local(): lax.all_to_all(answered, 'head', split_axis=0, concat_axis=0, tiled=True)  47.5 us
    ppermute x6, waiting for transfers between devices, partner_2(): return lax.ppermute(value, 'head', pairs)  33.7 us
    ppermute x2, waiting for transfers between devices, turn_grp(): lax.ppermute(value, 'grp', [(i, (i + shift) % count) for i in range(count)])  26.7 us
    pallas_call x1, Pallas kernels, attend(): pl.pallas_call(functools.partial(attend_kernel, block=block, old_block=ol...  19.2 us
    all_to_all x1, starting transfers between devices, local(): lax.all_to_all(query_slots, 'head', split_axis=0, concat_axis=0, tiled=True)  7.7 us
    dot_general x3, matrix products, local(): jnp.dot(term.astype(jnp.bfloat16), picked, preferred_element_type=jnp.flo...  7.31 us
  transfers between devices with their start and end apart: 12, of which 9 were waited for; matrix products, arithmetic and copies ran while one was open for 5% of the time, Pallas kernels for 6%

profile of v4, /device:TPU:13, one launch (start us, length us, event | category | flops | bytes accessed | tf_op | source)
XLA Modules:
  0.0 319.9 jit_solution(2473923982619349138)
XLA Ops:
  6.5 1.8 copy.41
  8.4 3.6 %all-to-all-start = ((bf16[2,128,512]{2,1,0:T(8,128)(2,1)}), bf16[2,128,512]{2,1,0:T(8,128)(2,1)S(1)}, u32[]{:S(2)}, u32[]{:S(2)}) async-start(bf16[2,128,512]{2,1,0:T(8,128)(2,1)} %bitcast.105), calls=%async_computation | async-start | bytes 524288 | tf_op jit(solution)/shard_map/all_to_all | solution.py:126
  11.9 2.6 copy.40
  14.5 3.6 %all-to-all-done = bf16[2,128,512]{2,1,0:T(8,128)(2,1)S(1)} async-done(((bf16[2,128,512]{2,1,0:T(8,128)(2,1)}), bf16[2,128,512]{2,1,0:T(8,128)(2,1)S(1)}, u32[]{:S(2)}, u32[]{:S(2)}) %all-to-all-start) | async-done | bytes 262176 | tf_op jit(solution)/shard_map/all_to_all | solution.py:126
  18.2 7.7 %all-to-all-start.1 = ((bf16[16,128,256]{2,1,0:T(8,128)(2,1)}), bf16[16,128,256]{2,1,0:T(8,128)(2,1)}, u32[]{:S(2)}, u32[]{:S(2)}) async-start(bf16[16,128,256]{2,1,0:T(8,128)(2,1)} %bitcast.104), calls=%async_computation.1 | async-start | bytes 2097152 | tf_op jit(solution)/shard_map/all_to_all | solution.py:139
  27.5 12.3 %collective-permute-done.2 = bf16[256,512]{1,0:T(8,128)(2,1)S(1)} collective-permute-done((bf16[256,512]{1,0:T(8,128)(2,1)S(1)}, bf16[256,512]{1,0:T(8,128)(2,1)S(1)}, u32[]{:S(2)}, u32[]{:S(2)}) %collective-permute-start.2) | collective-permute-done | bytes 262176 | tf_op jit(solution)/shard_map/ppermute | solution.py:16
  39.8 1.5 collective-permute-start.3
  41.3 6.9 %collective-permute-done = bf16[1,2,128,512]{3,2,1,0:T(8,128)(2,1)S(1)} collective-permute-done((bf16[1,2,128,512]{3,2,1,0:T(8,128)(2,1)S(1)}, bf16[1,2,128,512]{3,2,1,0:T(8,128)(2,1)S(1)}, u32[]{:S(2)}, u32[]{:S(2)}) %collective-permute-start) | collective-permute-done | bytes 262176 | tf_op jit(solution)/shard_map/ppermute | solution.py:16
  49.7 1.4 collective-permute-start.1
  51.2 1.9 constant_dynamic-slice_fusion
  53.1 2.9 collective-permute-done.3
  56.0 2.1 pad_maximum_fusion.2.cache_ref
  58.1 9.2 %collective-permute-done.1 = bf16[2,2,128,512]{3,2,1,0:T(8,128)(2,1)} collective-permute-done((bf16[2,2,128,512]{3,2,1,0:T(8,128)(2,1)}, bf16[2,2,128,512]{3,2,1,0:T(8,128)(2,1)}, u32[]{:S(2)}, u32[]{:S(2)}) %collective-permute-start.1) | collective-permute-done | bytes 524320 | tf_op jit(solution)/shard_map/ppermute | solution.py:16
  68.5 1.7 collective-permute-start.5
  70.3 2.3 collective-permute-done.5
  72.7 2.8 pad_maximum_fusion.pairs_ref
  75.4 19.2 %shard_map.100 = bf16[2048,256]{1,0:T(8,128)(2,1)} custom-call(s32[1]{0:T(128)} %bitcast.1.me_ref, bf16[2048,256]{1,0:T(8,128)(2,1)} %bitcast.8.query_ref, bf16[1024,512]{1,0:T(8,128)(2,1)} %pad_maximum_fusion.2.cache_ref, bf16[1024,512]{1,0:T(8,128)(2,1)} %collective-permute-done.4.other_ref, bf16[8,2,128,512]{3,2,1,0:T(8,128)(2,1)} %pad_maximum_fusion.pairs_ref), custom_call_target="tpu_custom_call" | custom-call | flops 6442450944 | bytes 8388608 | tf_op jit(solution)/shard_map/pallas_call | solution.py:89
  94.6 2.3 copy.29
  96.9 59.4 %all_to_all.25 = bf16[16,128,256]{1,2,0:T(8,128)(2,1)S(1)} all-to-all(bf16[16,128,256]{1,2,0:T(8,128)(2,1)} %copy.29), channel_id=1, replica_groups=mesh['grp'=2,'head'=16] {'head'}, dimensions={0} | all-to-all | bytes 2097152 | tf_op jit(solution)/shard_map/all_to_all | solution.py:153
  159.3 21.7 %collective-permute-done.6 = bf16[128,4096]{0,1:T(8,128)(2,1)} collective-permute-done((bf16[128,4096]{0,1:T(8,128)(2,1)S(1)}, bf16[128,4096]{0,1:T(8,128)(2,1)}, u32[]{:S(2)}, u32[]{:S(2)}) %collective-permute-start.6) | collective-permute-done | bytes 1048608 | tf_op jit(solution)/shard_map/ppermute | solution.py:21
  180.9 5.1 %convolution_convert_fusion.2 = bf16[128,1024]{1,0:T(8,128)(2,1)S(1)} fusion(bf16[128,4096]{0,1:T(8,128)(2,1)} %collective-permute-done.6, bf16[4096,1024]{1,0:T(8,128)(2,1)} %bitcast.106), kind=kOutput, calls=%fused_computation.14 | convolution fusion | flops 1073872896 | bytes 9699328 | tf_op jit(solution)/shard_map/dot_general | solution.py:165
  186.1 1.3 collective-permute-start.7
  187.4 1.3 fusion.50
  188.7 5.0 %collective-permute-done.7 = bf16[128,1024]{1,0:T(8,128)(2,1)S(1)} collective-permute-done((bf16[128,1024]{1,0:T(8,128)(2,1)S(1)}, bf16[128,1024]{1,0:T(8,128)(2,1)S(1)}, u32[]{:S(2)}, u32[]{:S(2)}) %collective-permute-start.7) | collective-permute-done | bytes 262176 | tf_op jit(solution)/shard_map/ppermute | solution.py:21
  194.9 53.1 %all_to_all.26 = bf16[16,1,32,2048]{3,2,1,0:T(8,128)(2,1)S(1)} all-to-all(bf16[16,1,32,2048]{3,2,1,0:T(8,128)(2,1)S(1)} %bitcast.108), channel_id=1, replica_groups=mesh['grp'=2,'head'=16] {'head'}, dimensions={0} | all-to-all | bytes 4194304 | tf_op jit(solution)/shard_map/all_to_all | solution.py:204
  248.1 2.4 fusion.8
  250.4 2.6 fusion.2
  253.1 5.2 %all-to-all-start.4 = ((bf16[16,1,32,2048]{3,2,1,0:T(8,128)(2,1)}), bf16[16,1,32,2048]{3,2,1,0:T(8,128)(2,1)}, u32[]{:S(2)}, u32[]{:S(2)}) async-start(bf16[16,1,32,2048]{3,2,1,0:T(8,128)(2,1)} %fusion.2), calls=%async_computation.4 | async-start | bytes 4194304 | tf_op jit(solution)/shard_map/all_to_all | solution.py:214
  258.2 47.5 %all-to-all-done.4 = bf16[16,1,32,2048]{3,2,1,0:T(8,128)(2,1)} async-done(((bf16[16,1,32,2048]{3,2,1,0:T(8,128)(2,1)}), bf16[16,1,32,2048]{3,2,1,0:T(8,128)(2,1)}, u32[]{:S(2)}, u32[]{:S(2)}) %all-to-all-start.4) | async-done | bytes 2097184 | tf_op jit(solution)/shard_map/all_to_all | solution.py:214
  305.8 2.1 fusion.23
  307.9 2.2 convolution_add_fusion.1
  310.1 3.0 fusion.5
  (51 shorter events, 8.5 us)
Async XLA Ops:
  6.5 243.9 %copy-start = (bf16[1,512,2048]{2,1,0:T(8,128)(2,1)S(1)}, bf16[1,512,2048]{2,1,0:T(8,128)(2,1)}, u32[]{:S(2)}) copy-start(bf16[1,512,2048]{2,1,0:T(8,128)(2,1)} %param.19) | copy-start | bytes 6291460
  8.4 9.8 %all-to-all-start = ((bf16[2,128,512]{2,1,0:T(8,128)(2,1)}), bf16[2,128,512]{2,1,0:T(8,128)(2,1)S(1)}, u32[]{:S(2)}, u32[]{:S(2)}) async-start(bf16[2,128,512]{2,1,0:T(8,128)(2,1)} %bitcast.105), calls=%async_computation | async-start | bytes 524288 | tf_op jit(solution)/shard_map/all_to_all | solution.py:126
  11.9 14.0 %copy-start.4 = (bf16[1,256,512]{2,1,0:T(8,128)(2,1)S(1)}, bf16[1,256,512]{2,1,0:T(8,128)(2,1)}, u32[]{:S(2)}) copy-start(bf16[1,256,512]{2,1,0:T(8,128)(2,1)} %param.12) | copy-start | bytes 786436
  18.2 50.3 %all-to-all-start.1 = ((bf16[16,128,256]{2,1,0:T(8,128)(2,1)}), bf16[16,128,256]{2,1,0:T(8,128)(2,1)}, u32[]{:S(2)}, u32[]{:S(2)}) async-start(bf16[16,128,256]{2,1,0:T(8,128)(2,1)} %bitcast.104), calls=%async_computation.1 | async-start | bytes 2097152 | tf_op jit(solution)/shard_map/all_to_all | solution.py:139
  25.9 155.1 %all-gather.2.cloned.1.call-start = ((), (), s32[]{:S(2)}) async-start(), calls=%async_computation.5 | async-start | bytes 8912896 | tf_op jit(solution)/shard_map/all_gather | solution.py:145
  25.9 13.8 %collective-permute-start.2 = (bf16[256,512]{1,0:T(8,128)(2,1)S(1)}, bf16[256,512]{1,0:T(8,128)(2,1)S(1)}, u32[]{:S(2)}, u32[]{:S(2)}) collective-permute-start(bf16[256,512]{1,0:T(8,128)(2,1)S(1)} %bitcast.115), channel_id=1, source_target_pairs={{0,2},{1,3},{2,0},{3,1},{4,6},{5,7},{6,4},{7,5},{8,10},{9,11},{10,... | collective-permute-start | bytes 786440 | tf_op jit(solution)/shard_map/ppermute | solution.py:16
  26.3 21.9 %collective-permute-start = (bf16[1,2,128,512]{3,2,1,0:T(8,128)(2,1)S(1)}, bf16[1,2,128,512]{3,2,1,0:T(8,128)(2,1)S(1)}, u32[]{:S(2)}, u32[]{:S(2)}) collective-permute-start(bf16[1,2,128,512]{3,2,1,0:T(8,128)(2,1)S(1)} %bitcast.111), channel_id=1, source_target_pairs={{0,2},{1,3},{2,0},{3,1},{4,6},{5,7},{6,4},{7,5},{8,10},{9,11},{10,... | collective-permute-start | bytes 786440 | tf_op jit(solution)/shard_map/ppermute | solution.py:16
  39.8 16.2 %collective-permute-start.3 = (bf16[512,512]{1,0:T(8,128)(2,1)S(1)}, bf16[512,512]{1,0:T(8,128)(2,1)}, u32[]{:S(2)}, u32[]{:S(2)}) collective-permute-start(bf16[512,512]{1,0:T(8,128)(2,1)S(1)} %pad_maximum_fusion.4), channel_id=1, source_target_pairs={{0,4},{1,5},{2,6},{3,7},{4,0},{5,1},{6,2},{7,3},{8,12},{9,13},{10,... | collective-permute-start | bytes 1572872 | tf_op jit(solution)/shard_map/ppermute | solution.py:16
  48.2 0.7 copy-start.5
  49.7 17.6 %collective-permute-start.1 = (bf16[2,2,128,512]{3,2,1,0:T(8,128)(2,1)}, bf16[2,2,128,512]{3,2,1,0:T(8,128)(2,1)}, u32[]{:S(2)}, u32[]{:S(2)}) collective-permute-start(bf16[2,2,128,512]{3,2,1,0:T(8,128)(2,1)} %pad_maximum_fusion.3), channel_id=1, source_target_pairs={{0,4},{1,5},{2,6},{3,7},{4,0},{5,1},{6,2},{7,3},{8,12},{9,13},{10,... | collective-permute-start | bytes 1572872 | tf_op jit(solution)/shard_map/ppermute | solution.py:16
  53.1 14.3 %copy-start.6 = (bf16[1,2,128,512]{3,2,1,0:T(8,128)(2,1)S(1)}, bf16[1,2,128,512]{3,2,1,0:T(8,128)(2,1)}, u32[]{:S(2)}) copy-start(bf16[1,2,128,512]{3,2,1,0:T(8,128)(2,1)} %copy-done.5) | copy-start | bytes 786436
  68.5 4.1 %collective-permute-start.5 = (bf16[4,2,128,512]{3,2,1,0:T(8,128)(2,1)S(1)}, bf16[4,2,128,512]{3,2,1,0:T(8,128)(2,1)}, u32[]{:S(2)}, u32[]{:S(2)}) collective-permute-start(bf16[4,2,128,512]{3,2,1,0:T(8,128)(2,1)S(1)} %pad_maximum_fusion.1), channel_id=1, source_target_pairs={{0,1},{1,0},{2,3},{3,2},{4,5},{5,4},{6,7},{7,6},{8,9},{9,8},{10,11... | collective-permute-start | bytes 3145736 | tf_op jit(solution)/shard_map/ppermute | solution.py:16
  70.2 5.2 %collective-permute-start.4 = (bf16[1024,512]{1,0:T(8,128)(2,1)}, bf16[1024,512]{1,0:T(8,128)(2,1)}, u32[]{:S(2)}, u32[]{:S(2)}) collective-permute-start(bf16[1024,512]{1,0:T(8,128)(2,1)} %pad_maximum_fusion.2.cache_ref), channel_id=1, source_target_pairs={{0,1},{1,0},{2,3},{3,2},{4,5},{5,4},{6,7},{7,6},{8,9},{9,8},{10,11... | collective-permute-start | bytes 3145736 | tf_op jit(solution)/shard_map/ppermute | solution.py:16
  94.6 63.0 %copy-start.8 = (s32[128,1,2]{0,2,1:T(2,128)S(1)}, s32[128,1,2]{0,2,1:T(2,128)}, u32[]{:S(2)}) copy-start(s32[128,1,2]{0,2,1:T(2,128)} %param.16) | copy-start | bytes 3076
  156.4 24.6 %collective-permute-start.6 = (bf16[128,4096]{0,1:T(8,128)(2,1)S(1)}, bf16[128,4096]{0,1:T(8,128)(2,1)}, u32[]{:S(2)}, u32[]{:S(2)}) collective-permute-start(bf16[128,4096]{0,1:T(8,128)(2,1)S(1)} %bitcast.109), channel_id=1, source_target_pairs={{0,16},{16,0},{1,17},{17,1},{2,18},{18,2},{3,19},{19,3},{4,20},{20... | collective-permute-start | bytes 3145736 | tf_op jit(solution)/shard_map/ppermute | solution.py:21
  180.9 6.4 %copy-start.1 = (bf16[16,256,1024]{2,1,0:T(8,128)(2,1)S(1)}, bf16[16,256,1024]{2,1,0:T(8,128)(2,1)}, u32[]{:S(2)}) copy-start(bf16[16,256,1024]{2,1,0:T(8,128)(2,1)} %all-gather.2.cloned.1.call-done) | copy-start | bytes 25165828
  186.1 7.7 %collective-permute-start.7 = (bf16[128,1024]{1,0:T(8,128)(2,1)S(1)}, bf16[128,1024]{1,0:T(8,128)(2,1)S(1)}, u32[]{:S(2)}, u32[]{:S(2)}) collective-permute-start(bf16[128,1024]{1,0:T(8,128)(2,1)S(1)} %convolution_convert_fusion.2), channel_id=1, source_target_pairs={{0,16},{16,0},{1,17},{17,1},{2,18},{18,2},{3,19},{19,3},{4,20},{20... | collective-permute-start | bytes 786440 | tf_op jit(solution)/shard_map/ppermute | solution.py:21
  188.7 5.1 %copy-start.2 = (bf16[128,1,2048]{2,0,1:T(8,128)(2,1)S(1)}, bf16[128,1,2048]{2,0,1:T(8,128)(2,1)}, u32[]{:S(2)}) copy-start(bf16[128,1,2048]{2,0,1:T(8,128)(2,1)} %param.13) | copy-start | bytes 1572868
  188.7 5.4 %copy-start.7 = (f32[2048]{0:T(1024)S(1)}, f32[2048]{0:T(1024)}, u32[]{:S(2)}) copy-start(f32[2048]{0:T(1024)} %param.15) | copy-start | bytes 24580
  194.9 53.2 %copy-start.10 = (bf16[1,2048,1024]{2,1,0:T(8,128)(2,1)S(1)}, bf16[1,2048,1024]{2,1,0:T(8,128)(2,1)}, u32[]{:S(2)}) copy-start(bf16[1,2048,1024]{2,1,0:T(8,128)(2,1)} %param.18) | copy-start | bytes 12582916
  253.1 5.2 %copy-start.9 = (f32[128,1,2]{0,2,1:T(2,128)S(1)}, f32[128,1,2]{0,2,1:T(2,128)}, u32[]{:S(2)}) copy-start(f32[128,1,2]{0,2,1:T(2,128)} %param.17) | copy-start | bytes 3076
  253.1 52.7 %all-to-all-start.4 = ((bf16[16,1,32,2048]{3,2,1,0:T(8,128)(2,1)}), bf16[16,1,32,2048]{3,2,1,0:T(8,128)(2,1)}, u32[]{:S(2)}, u32[]{:S(2)}) async-start(bf16[16,1,32,2048]{3,2,1,0:T(8,128)(2,1)} %fusion.2), calls=%async_computation.4 | async-start | bytes 4194304 | tf_op jit(solution)/shard_map/all_to_all | solution.py:214
  307.9 2.2 copy-start.3
Sparse Core Ops, SparseCore 0:
  68.7 94.4 all-gather.1

commit v5 on v4

--- a/solution.py
+++ b/solution.py
@@ -139,9 +139,7 @@
     head_queries = lax.all_to_all(query_slots, "head", split_axis=0, concat_axis=0, tiled=True)
     for bit in order[:-1]:
         pairs = jnp.concatenate([pairs, partner_2(pairs, bit)], 0)
-    w_part, pairs, cache_rows, head_queries = lax.optimization_barrier(
-        (w_part, pairs, cache_rows, head_queries)
-    )
+    w_part, pairs, cache_rows = lax.optimization_barrier((w_part, pairs, cache_rows))
     w_part = lax.all_gather(w_part, "head", axis=1, tiled=True)
     w_part = w_part.reshape(head_count * head_width, part_width)
     cache_other = partner_2(cache_rows, 0)

time: 321 us -> 326 us (1.016)
  waiting for transfers between devices: 112 us -> 134 us
  blocking collectives: 113 us -> 95.5 us
    all_to_all x1, waiting for transfers between devices: 0.01 us -> 36.1 us  [local(): lax.all_to_all(query_slots, 'head', split_axis=0, concat_axis=0, tiled=True)]
    all_to_all x1, blocking collectives: 59.4 us -> 41.1 us  [local(): lax.all_to_all(attended.reshape(axis_count, local_rows, head_width), 'hea...]
    ppermute x6, waiting for transfers between devices: 33.7 us -> 18.5 us  [partner_2(): return lax.ppermute(value, 'head', pairs)]
  transfers between devices with their start and end apart: 12 -> 12, of which waited for: 9 -> 10; matrix products, arithmetic and copies ran while one was open for 5% -> 5% of each run, Pallas kernels for 6% -> 6%
where the time goes in v5:
time: 326 us; the launch traced here: 325 us
  waiting for transfers between devices  134 us (41%)
  blocking collectives  95.5 us (29%)
  starting transfers between devices  24.3 us (7%)
  matrix products  19.6 us (6%)
  Pallas kernels  19.1 us (6%)
  between operations  13.6 us (4%)
  other arithmetic  9.87 us (3%)
  local copies, waits for them, and re-layouts  9.53 us (3%)
    all_to_all x1, blocking collectives, local(): lax.all_to_all(outgoing, 'head', split_axis=0, concat_axis=0, tiled=True)  54.3 us
    all_to_all x1, waiting for transfers between devices, local(): lax.all_to_all(answered, 'head', split_axis=0, concat_axis=0, tiled=True)  47.5 us
    all_to_all x1, blocking collectives, local(): lax.all_to_all(attended.reshape(axis_count, local_rows, head_width), 'hea...  41.1 us
    all_to_all x1, waiting for transfers between devices, local(): lax.all_to_all(query_slots, 'head', split_axis=0, concat_axis=0, tiled=True)  36.1 us
    ppermute x2, waiting for transfers between devices, turn_grp(): lax.ppermute(value, 'grp', [(i, (i + shift) % count) for i in range(count)])  25.7 us
    pallas_call x1, Pallas kernels, attend(): pl.pallas_call(functools.partial(attend_kernel, block=block, old_block=ol...  19.1 us
    ppermute x6, waiting for transfers between devices, partner_2(): return lax.ppermute(value, 'head', pairs)  18.5 us
    all_to_all x1, starting transfers between devices, local(): lax.all_to_all(query_slots, 'head', split_axis=0, concat_axis=0, tiled=True)  8.94 us
  transfers between devices with their start and end apart: 12, of which 10 were waited for; matrix products, arithmetic and copies ran while one was open for 5% of the time, Pallas kernels for 6%

profile of v5, /device:TPU:13, one launch (start us, length us, event | category | flops | bytes accessed | tf_op | source)
XLA Modules:
  0.0 325.2 jit_solution(16953809500218057984)
XLA Ops:
  6.5 1.8 copy.41
  8.4 3.6 %all-to-all-start.1 = ((bf16[2,128,512]{2,1,0:T(8,128)(2,1)}), bf16[2,128,512]{2,1,0:T(8,128)(2,1)S(1)}, u32[]{:S(2)}, u32[]{:S(2)}) async-start(bf16[2,128,512]{2,1,0:T(8,128)(2,1)} %bitcast.105), calls=%async_computation.1 | async-start | bytes 524288 | tf_op jit(solution)/shard_map/all_to_all | solution.py:126
  12.2 6.0 %all-to-all-done.1 = bf16[2,128,512]{2,1,0:T(8,128)(2,1)S(1)} async-done(((bf16[2,128,512]{2,1,0:T(8,128)(2,1)}), bf16[2,128,512]{2,1,0:T(8,128)(2,1)S(1)}, u32[]{:S(2)}, u32[]{:S(2)}) %all-to-all-start.1) | async-done | bytes 262176 | tf_op jit(solution)/shard_map/all_to_all | solution.py:126
  19.1 1.8 pad_maximum_fusion.4
  20.9 1.6 collective-permute-start.3
  22.4 2.7 collective-permute-done
  26.1 1.6 collective-permute-start.1
  27.7 1.9 constant_dynamic-slice_fusion
  29.6 3.5 %collective-permute-done.3 = bf16[512,512]{1,0:T(8,128)(2,1)} collective-permute-done((bf16[512,512]{1,0:T(8,128)(2,1)}, bf16[512,512]{1,0:T(8,128)(2,1)}, u32[]{:S(2)}, u32[]{:S(2)}) %collective-permute-start.3) | collective-permute-done | bytes 524320 | tf_op jit(solution)/shard_map/ppermute | solution.py:16
  33.1 2.1 pad_maximum_fusion.2.cache_ref
  35.2 9.1 %collective-permute-done.1 = bf16[2,2,128,512]{3,2,1,0:T(8,128)(2,1)} collective-permute-done((bf16[2,2,128,512]{3,2,1,0:T(8,128)(2,1)}, bf16[2,2,128,512]{3,2,1,0:T(8,128)(2,1)}, u32[]{:S(2)}, u32[]{:S(2)}) %collective-permute-start.1) | collective-permute-done | bytes 524320 | tf_op jit(solution)/shard_map/ppermute | solution.py:16
  45.6 2.5 copy.40
  48.1 8.9 %all-to-all-start = ((bf16[16,128,256]{2,1,0:T(8,128)(2,1)}), bf16[16,128,256]{2,1,0:T(8,128)(2,1)}, u32[]{:S(2)}, u32[]{:S(2)}) async-start(bf16[16,128,256]{2,1,0:T(8,128)(2,1)} %bitcast.104), calls=%async_computation | async-start | bytes 2097152 | tf_op jit(solution)/shard_map/all_to_all | solution.py:139
  57.6 2.5 collective-permute-done.5
  60.0 2.8 pad_maximum_fusion.pairs_ref
  62.8 36.1 %all-to-all-done = bf16[16,128,256]{2,1,0:T(8,128)(2,1)} async-done(((bf16[16,128,256]{2,1,0:T(8,128)(2,1)}), bf16[16,128,256]{2,1,0:T(8,128)(2,1)}, u32[]{:S(2)}, u32[]{:S(2)}) %all-to-all-start) | async-done | bytes 1048608 | tf_op jit(solution)/shard_map/all_to_all | solution.py:139
  98.9 19.1 %shard_map.100 = bf16[2048,256]{1,0:T(8,128)(2,1)} custom-call(s32[1]{0:T(128)} %bitcast.1.me_ref, bf16[2048,256]{1,0:T(8,128)(2,1)} %bitcast.4.query_ref, bf16[1024,512]{1,0:T(8,128)(2,1)} %pad_maximum_fusion.2.cache_ref, bf16[1024,512]{1,0:T(8,128)(2,1)} %collective-permute-done.4.other_ref, bf16[8,2,128,512]{3,2,1,0:T(8,128)(2,1)} %pad_maximum_fusion.pairs_ref), custom_call_target="tpu_custom_call" | custom-call | flops 6442450944 | bytes 8388608 | tf_op jit(solution)/shard_map/pallas_call | solution.py:89
  118.1 2.3 copy.29
  120.4 41.1 %all_to_all.25 = bf16[16,128,256]{1,2,0:T(8,128)(2,1)S(1)} all-to-all(bf16[16,128,256]{1,2,0:T(8,128)(2,1)} %copy.29), channel_id=1, replica_groups=mesh['grp'=2,'head'=16] {'head'}, dimensions={0} | all-to-all | bytes 2097152 | tf_op jit(solution)/shard_map/all_to_all | solution.py:151
  164.3 21.6 %collective-permute-done.6 = bf16[128,4096]{0,1:T(8,128)(2,1)} collective-permute-done((bf16[128,4096]{0,1:T(8,128)(2,1)S(1)}, bf16[128,4096]{0,1:T(8,128)(2,1)}, u32[]{:S(2)}, u32[]{:S(2)}) %collective-permute-start.6) | collective-permute-done | bytes 1048608 | tf_op jit(solution)/shard_map/ppermute | solution.py:21
  185.9 5.1 %convolution_convert_fusion.2 = bf16[128,1024]{1,0:T(8,128)(2,1)S(1)} fusion(bf16[128,4096]{0,1:T(8,128)(2,1)} %collective-permute-done.6, bf16[4096,1024]{1,0:T(8,128)(2,1)} %bitcast.106), kind=kOutput, calls=%fused_computation.14 | convolution fusion | flops 1073872896 | bytes 9699328 | tf_op jit(solution)/shard_map/dot_general | solution.py:163
  191.1 1.2 collective-permute-start.7
  192.3 1.3 fusion.50
  193.7 4.1 %collective-permute-done.7 = bf16[128,1024]{1,0:T(8,128)(2,1)S(1)} collective-permute-done((bf16[128,1024]{1,0:T(8,128)(2,1)S(1)}, bf16[128,1024]{1,0:T(8,128)(2,1)S(1)}, u32[]{:S(2)}, u32[]{:S(2)}) %collective-permute-start.7) | collective-permute-done | bytes 262176 | tf_op jit(solution)/shard_map/ppermute | solution.py:21
  199.0 54.3 %all_to_all.26 = bf16[16,1,32,2048]{3,2,1,0:T(8,128)(2,1)S(1)} all-to-all(bf16[16,1,32,2048]{3,2,1,0:T(8,128)(2,1)S(1)} %bitcast.108), channel_id=1, replica_groups=mesh['grp'=2,'head'=16] {'head'}, dimensions={0} | all-to-all | bytes 4194304 | tf_op jit(solution)/shard_map/all_to_all | solution.py:202
  253.3 2.4 fusion.8
  255.7 2.6 fusion.2
  258.3 5.2 %all-to-all-start.4 = ((bf16[16,1,32,2048]{3,2,1,0:T(8,128)(2,1)}), bf16[16,1,32,2048]{3,2,1,0:T(8,128)(2,1)}, u32[]{:S(2)}, u32[]{:S(2)}) async-start(bf16[16,1,32,2048]{3,2,1,0:T(8,128)(2,1)} %fusion.2), calls=%async_computation.4 | async-start | bytes 4194304 | tf_op jit(solution)/shard_map/all_to_all | solution.py:212
  263.5 47.5 %all-to-all-done.4 = bf16[16,1,32,2048]{3,2,1,0:T(8,128)(2,1)} async-done(((bf16[16,1,32,2048]{3,2,1,0:T(8,128)(2,1)}), bf16[16,1,32,2048]{3,2,1,0:T(8,128)(2,1)}, u32[]{:S(2)}, u32[]{:S(2)}) %all-to-all-start.4) | async-done | bytes 2097184 | tf_op jit(solution)/shard_map/all_to_all | solution.py:212
  311.0 2.1 fusion.23
  313.1 2.2 convolution_add_fusion.1
  315.3 3.0 fusion.5
  (49 shorter events, 7.8 us)
Async XLA Ops:
  6.5 249.2 %copy-start = (bf16[1,512,2048]{2,1,0:T(8,128)(2,1)S(1)}, bf16[1,512,2048]{2,1,0:T(8,128)(2,1)}, u32[]{:S(2)}) copy-start(bf16[1,512,2048]{2,1,0:T(8,128)(2,1)} %param.19) | copy-start | bytes 6291460
  6.5 26.6 %copy-start.4 = (bf16[1,256,512]{2,1,0:T(8,128)(2,1)S(1)}, bf16[1,256,512]{2,1,0:T(8,128)(2,1)}, u32[]{:S(2)}) copy-start(bf16[1,256,512]{2,1,0:T(8,128)(2,1)} %param.12) | copy-start | bytes 786436
  8.4 9.8 %all-to-all-start.1 = ((bf16[2,128,512]{2,1,0:T(8,128)(2,1)}), bf16[2,128,512]{2,1,0:T(8,128)(2,1)S(1)}, u32[]{:S(2)}, u32[]{:S(2)}) async-start(bf16[2,128,512]{2,1,0:T(8,128)(2,1)} %bitcast.105), calls=%async_computation.1 | async-start | bytes 524288 | tf_op jit(solution)/shard_map/all_to_all | solution.py:126
  12.0 174.0 %all-gather.2.cloned.1.call-start = ((), (), s32[]{:S(2)}) async-start(), calls=%async_computation.5 | async-start | bytes 8912896 | tf_op jit(solution)/shard_map/all_gather | solution.py:143
  12.0 7.1 %collective-permute-start.2 = (bf16[256,512]{1,0:T(8,128)(2,1)}, bf16[256,512]{1,0:T(8,128)(2,1)S(1)}, u32[]{:S(2)}, u32[]{:S(2)}) collective-permute-start(bf16[256,512]{1,0:T(8,128)(2,1)} %bitcast.115), channel_id=1, source_target_pairs={{0,2},{1,3},{2,0},{3,1},{4,6},{5,7},{6,4},{7,5},{8,10},{9,11},{10,... | collective-permute-start | bytes 786440 | tf_op jit(solution)/shard_map/ppermute | solution.py:16
  18.2 7.0 %collective-permute-start = (bf16[1,2,128,512]{3,2,1,0:T(8,128)(2,1)S(1)}, bf16[1,2,128,512]{3,2,1,0:T(8,128)(2,1)S(1)}, u32[]{:S(2)}, u32[]{:S(2)}) collective-permute-start(bf16[1,2,128,512]{3,2,1,0:T(8,128)(2,1)S(1)} %bitcast.111), channel_id=1, source_target_pairs={{0,2},{1,3},{2,0},{3,1},{4,6},{5,7},{6,4},{7,5},{8,10},{9,11},{10,... | collective-permute-start | bytes 786440 | tf_op jit(solution)/shard_map/ppermute | solution.py:16
  20.9 12.3 %collective-permute-start.3 = (bf16[512,512]{1,0:T(8,128)(2,1)}, bf16[512,512]{1,0:T(8,128)(2,1)}, u32[]{:S(2)}, u32[]{:S(2)}) collective-permute-start(bf16[512,512]{1,0:T(8,128)(2,1)} %pad_maximum_fusion.4), channel_id=1, source_target_pairs={{0,4},{1,5},{2,6},{3,7},{4,0},{5,1},{6,2},{7,3},{8,12},{9,13},{10,... | collective-permute-start | bytes 1572872 | tf_op jit(solution)/shard_map/ppermute | solution.py:16
  25.2 10.0 %copy-start.5 = (bf16[1,2,128,512]{3,2,1,0:T(8,128)(2,1)}, bf16[1,2,128,512]{3,2,1,0:T(8,128)(2,1)S(1)}, u32[]{:S(2)}) copy-start(bf16[1,2,128,512]{3,2,1,0:T(8,128)(2,1)S(1)} %collective-permute-done) | copy-start | bytes 786436
  26.1 18.3 %collective-permute-start.1 = (bf16[2,2,128,512]{3,2,1,0:T(8,128)(2,1)}, bf16[2,2,128,512]{3,2,1,0:T(8,128)(2,1)}, u32[]{:S(2)}, u32[]{:S(2)}) collective-permute-start(bf16[2,2,128,512]{3,2,1,0:T(8,128)(2,1)} %pad_maximum_fusion.3), channel_id=1, source_target_pairs={{0,4},{1,5},{2,6},{3,7},{4,0},{5,1},{6,2},{7,3},{8,12},{9,13},{10,... | collective-permute-start | bytes 1572872 | tf_op jit(solution)/shard_map/ppermute | solution.py:16
  48.1 50.8 %all-to-all-start = ((bf16[16,128,256]{2,1,0:T(8,128)(2,1)}), bf16[16,128,256]{2,1,0:T(8,128)(2,1)}, u32[]{:S(2)}, u32[]{:S(2)}) async-start(bf16[16,128,256]{2,1,0:T(8,128)(2,1)} %bitcast.104), calls=%async_computation | async-start | bytes 2097152 | tf_op jit(solution)/shard_map/all_to_all | solution.py:139
  57.1 3.0 collective-permute-start.5
  57.5 41.5 %collective-permute-start.4 = (bf16[1024,512]{1,0:T(8,128)(2,1)}, bf16[1024,512]{1,0:T(8,128)(2,1)}, u32[]{:S(2)}, u32[]{:S(2)}) collective-permute-start(bf16[1024,512]{1,0:T(8,128)(2,1)} %pad_maximum_fusion.2.cache_ref), channel_id=1, source_target_pairs={{0,1},{1,0},{2,3},{3,2},{4,5},{5,4},{6,7},{7,6},{8,9},{9,8},{10,11... | collective-permute-start | bytes 3145736 | tf_op jit(solution)/shard_map/ppermute | solution.py:16
  118.1 44.6 %copy-start.7 = (s32[128,1,2]{0,2,1:T(2,128)S(1)}, s32[128,1,2]{0,2,1:T(2,128)}, u32[]{:S(2)}) copy-start(s32[128,1,2]{0,2,1:T(2,128)} %param.16) | copy-start | bytes 3076
  161.5 24.5 %collective-permute-start.6 = (bf16[128,4096]{0,1:T(8,128)(2,1)S(1)}, bf16[128,4096]{0,1:T(8,128)(2,1)}, u32[]{:S(2)}, u32[]{:S(2)}) collective-permute-start(bf16[128,4096]{0,1:T(8,128)(2,1)S(1)} %bitcast.109), channel_id=1, source_target_pairs={{0,16},{16,0},{1,17},{17,1},{2,18},{18,2},{3,19},{19,3},{4,20},{20... | collective-permute-start | bytes 3145736 | tf_op jit(solution)/shard_map/ppermute | solution.py:21
  185.9 6.4 %copy-start.1 = (bf16[16,256,1024]{2,1,0:T(8,128)(2,1)S(1)}, bf16[16,256,1024]{2,1,0:T(8,128)(2,1)}, u32[]{:S(2)}) copy-start(bf16[16,256,1024]{2,1,0:T(8,128)(2,1)} %all-gather.2.cloned.1.call-done) | copy-start | bytes 25165828
  191.1 6.7 %collective-permute-start.7 = (bf16[128,1024]{1,0:T(8,128)(2,1)S(1)}, bf16[128,1024]{1,0:T(8,128)(2,1)S(1)}, u32[]{:S(2)}, u32[]{:S(2)}) collective-permute-start(bf16[128,1024]{1,0:T(8,128)(2,1)S(1)} %convolution_convert_fusion.2), channel_id=1, source_target_pairs={{0,16},{16,0},{1,17},{17,1},{2,18},{18,2},{3,19},{19,3},{4,20},{20... | collective-permute-start | bytes 786440 | tf_op jit(solution)/shard_map/ppermute | solution.py:21
  193.7 4.2 %copy-start.2 = (bf16[128,1,2048]{2,0,1:T(8,128)(2,1)S(1)}, bf16[128,1,2048]{2,0,1:T(8,128)(2,1)}, u32[]{:S(2)}) copy-start(bf16[128,1,2048]{2,0,1:T(8,128)(2,1)} %param.13) | copy-start | bytes 1572868
  193.7 4.5 %copy-start.6 = (f32[2048]{0:T(1024)S(1)}, f32[2048]{0:T(1024)}, u32[]{:S(2)}) copy-start(f32[2048]{0:T(1024)} %param.15) | copy-start | bytes 24580
  199.0 54.4 %copy-start.9 = (bf16[1,2048,1024]{2,1,0:T(8,128)(2,1)S(1)}, bf16[1,2048,1024]{2,1,0:T(8,128)(2,1)}, u32[]{:S(2)}) copy-start(bf16[1,2048,1024]{2,1,0:T(8,128)(2,1)} %param.18) | copy-start | bytes 12582916
  258.3 5.2 %copy-start.8 = (f32[128,1,2]{0,2,1:T(2,128)S(1)}, f32[128,1,2]{0,2,1:T(2,128)}, u32[]{:S(2)}) copy-start(f32[128,1,2]{0,2,1:T(2,128)} %param.17) | copy-start | bytes 3076
  258.3 52.7 %all-to-all-start.4 = ((bf16[16,1,32,2048]{3,2,1,0:T(8,128)(2,1)}), bf16[16,1,32,2048]{3,2,1,0:T(8,128)(2,1)}, u32[]{:S(2)}, u32[]{:S(2)}) async-start(bf16[16,1,32,2048]{3,2,1,0:T(8,128)(2,1)} %fusion.2), calls=%async_computation.4 | async-start | bytes 4194304 | tf_op jit(solution)/shard_map/all_to_all | solution.py:212
  313.1 2.2 copy-start.3
Sparse Core Ops, SparseCore 0:
  45.7 107.9 all-gather.1
